TPU v7x, 768 devices: a whole 4x8x12 slice. The times are simulated.
768 devices in a mesh: pipe: 192 (over z, y, core), tensor: 4 (over x).
Axes of the slice: x: 4, y: 8, z: 12, core: 2. Of those that a mesh axis runs over, the one named last changes fastest.
Arguments:
- query: bfloat16 [49152, 2048], P(('pipe', 'tensor')), may hold values from -20 to 20
- key: bfloat16 [49152, 1024], P(('pipe', 'tensor')), may hold values from -20 to 20
- value: bfloat16 [49152, 1024], P(('pipe', 'tensor')), may hold values from -6 to 6
- grad_out: bfloat16 [49152, 2048], P(('pipe', 'tensor')), may hold values from -6 to 6
- segment_ids: int32 [49152], replicated, may hold values from 0 to 47, never falling along the last dimension, each value on 1 to 2048 neighbouring positions
Outputs:
- attn_out: bfloat16 [49152, 2048], P(('pipe', 'tensor'))
- grad_query: bfloat16 [49152, 2048], P(('pipe', 'tensor'))
- grad_key: bfloat16 [49152, 1024], P(('pipe', 'tensor'))
- grad_value: bfloat16 [49152, 1024], P(('pipe', 'tensor'))
Inputs may be any that keep to these rules, and one draw needn't show every extreme that they name: `segment_ids`: segment ids never fall along the tokens; each of the 48 documents holds 1 to 2048 tokens and one holds exactly 2048.
All inputs are finite; a program needn't handle non-finite values.
Results may differ from a plain program's by a relative error of at most 0.029.
Values may be sent and summed in bfloat16 or wider, within the bound.
A program may use at most 32 MiB of HBM per device.

v0:
```python
import jax
import jax.numpy as jnp
from jax import lax
from jax.sharding import PartitionSpec as P

HEAD_DIM = 128
WINDOW = 1024


logit_scale = 168.0 ** (-0.5)


def shifted(value, axis, steps):
    count = lax.axis_size(axis)
    initial, last = (max(0, -steps), min(count, count - steps))
    return lax.ppermute(value, axis, [(source, source + steps) for source in range(initial, last)])


def tile_allowed(segment_ids, index, lag, tok):
    q_start = index * tok
    k_start = (index - lag) * tok
    q_seg = lax.dynamic_slice_in_dim(segment_ids, q_start, tok, 0)
    k_seg = lax.dynamic_slice_in_dim(segment_ids, jnp.maximum(k_start, 0), tok, 0)
    offsets = jnp.arange(tok, dtype=jnp.int32)
    k_pos = k_start + offsets
    distance = (q_start + offsets)[:, None] - k_pos[None, :]
    return (
        (k_pos[None, :] >= 0)
        & (distance >= 0)
        & (distance < WINDOW)
        & (q_seg[:, None] == k_seg[None, :])
    )


def body(query, key, value, grad_out, segment_ids):
    q_rows, k_rows, v_rows, g_rows = (
        lax.all_to_all(query, "tensor", split_axis=1, concat_axis=0, tiled=True),
        lax.all_to_all(key, "tensor", split_axis=1, concat_axis=0, tiled=True),
        lax.all_to_all(value, "tensor", split_axis=1, concat_axis=0, tiled=True),
        lax.all_to_all(grad_out, "tensor", split_axis=1, concat_axis=0, tiled=True),
    )
    tok = q_rows.shape[0]
    kv_local = k_rows.shape[1] // HEAD_DIM
    group = q_rows.shape[1] // k_rows.shape[1]
    reach = WINDOW // tok
    index = lax.axis_index("pipe")
    grouped_queries = jnp.transpose(q_rows.reshape(tok, kv_local, group, HEAD_DIM), (1, 2, 0, 3))
    grouped_output_gradient = jnp.transpose(
        g_rows.reshape(tok, kv_local, group, HEAD_DIM), (1, 2, 0, 3)
    )
    kv_pair = jnp.stack((k_rows, v_rows))
    tiles = [kv_pair]
    for lag in range(1, reach + 1):
        tiles.append(shifted(kv_pair, "pipe", lag))
    masks = [tile_allowed(segment_ids, index, lag, tok) for lag in range(reach + 1)]
    scores = []
    for lag in range(reach + 1):
        raw_key_tensor = tiles[lag][0].reshape(tok, kv_local, HEAD_DIM)
        part = (
            jnp.einsum(
                "pmcz,fpz->pmcf",
                grouped_queries,
                raw_key_tensor,
                preferred_element_type=jnp.float32,
            )
            * logit_scale
        )
        scores.append(jnp.where(masks[lag], part, -jnp.inf))
    top = jnp.max(scores[0], axis=-1, keepdims=True)
    for part in scores[1:]:
        top = jnp.maximum(top, jnp.max(part, axis=-1, keepdims=True))
    expos = [jnp.exp(part - top) for part in scores]
    denominator_sum = jnp.sum(expos[0], axis=-1, keepdims=True)
    for part in expos[1:]:
        denominator_sum = denominator_sum + jnp.sum(part, axis=-1, keepdims=True)
    out_shape = (kv_local, group, tok, HEAD_DIM)
    summed = jnp.zeros(out_shape, jnp.float32)
    for lag in range(reach + 1):
        weighted_value_tensor = tiles[lag][1].reshape(tok, kv_local, HEAD_DIM)
        summed = summed + jnp.einsum(
            "xypq,qxa->xypa",
            expos[lag].astype(jnp.bfloat16),
            weighted_value_tensor,
            preferred_element_type=jnp.float32,
        )
    out_half = (summed / denominator_sum).astype(jnp.bfloat16)
    delta = jnp.sum(
        grouped_output_gradient.astype(jnp.float32) * out_half.astype(jnp.float32),
        axis=-1,
        keepdims=True,
    )
    dq_sum = jnp.zeros(out_shape, jnp.float32)
    kv_terms = []
    for lag in range(reach + 1):
        key_tensor = tiles[lag][0].reshape(tok, kv_local, HEAD_DIM)
        value_tensor = tiles[lag][1].reshape(tok, kv_local, HEAD_DIM)
        probabilities = expos[lag] / denominator_sum
        probability_gradient = jnp.einsum(
            "pmcz,fpz->pmcf",
            grouped_output_gradient,
            value_tensor,
            preferred_element_type=jnp.float32,
        )
        score_gradient = (probabilities * (probability_gradient - delta)).astype(jnp.bfloat16)
        query_gradient_term = jnp.einsum(
            "xypq,qxa->xypa", score_gradient, key_tensor, preferred_element_type=jnp.float32
        )
        dk_term = (
            jnp.einsum(
                "ihjm,ihjx->mix",
                score_gradient,
                grouped_queries,
                preferred_element_type=jnp.float32,
            )
            * logit_scale
        )
        dv_term = jnp.einsum(
            "ihjm,ihjx->mix",
            probabilities.astype(jnp.bfloat16),
            grouped_output_gradient,
            preferred_element_type=jnp.float32,
        )
        query_gradient_term, kv_term = (
            query_gradient_term,
            jnp.stack(
                (
                    dk_term.reshape(tok, kv_local * HEAD_DIM),
                    dv_term.reshape(tok, kv_local * HEAD_DIM),
                )
            ),
        )
        dq_sum = dq_sum + query_gradient_term
        kv_terms.append(kv_term)
    kv_grad = kv_terms[0]
    for lag in range(1, reach + 1):
        kv_grad = kv_grad + shifted(kv_terms[lag].astype(jnp.bfloat16), "pipe", -lag).astype(
            jnp.float32
        )
    out_rows = jnp.transpose(out_half, (2, 0, 1, 3)).reshape(tok, kv_local * group * HEAD_DIM)
    grad_q_rows = (
        jnp.transpose(dq_sum * logit_scale, (2, 0, 1, 3))
        .reshape(tok, kv_local * group * HEAD_DIM)
        .astype(jnp.bfloat16)
    )
    grad_k_rows = kv_grad[0].astype(jnp.bfloat16)
    grad_v_rows = kv_grad[1].astype(jnp.bfloat16)
    attn_out, grad_query, grad_key, grad_value = (
        lax.all_to_all(out_rows, "tensor", split_axis=0, concat_axis=1, tiled=True),
        lax.all_to_all(grad_q_rows, "tensor", split_axis=0, concat_axis=1, tiled=True),
        lax.all_to_all(grad_k_rows, "tensor", split_axis=0, concat_axis=1, tiled=True),
        lax.all_to_all(grad_v_rows, "tensor", split_axis=0, concat_axis=1, tiled=True),
    )
    return (attn_out, grad_query, grad_key, grad_value)


def solution(mesh):
    placed = (
        P(("pipe", "tensor"), None),
        P(("pipe", "tensor"), None),
        P(("pipe", "tensor"), None),
        P(("pipe", "tensor"), None),
        P(),
    )
    return jax.shard_map(
        body,
        mesh=mesh,
        in_specs=placed,
        out_specs=(
            P(("pipe", "tensor"), None),
            P(("pipe", "tensor"), None),
            P(("pipe", "tensor"), None),
            P(("pipe", "tensor"), None),
        ),
        check_vma=False,
    )
```

profile of v0, /device:TPU:240, one launch (start us, length us, event | category | flops | bytes accessed | tf_op | source)
XLA Modules:
  0.0 164.9 jit_solution(4862909170383520533)
XLA Ops:
  2.3 4.3 %all-to-all-start.1 = ((bf16[64,4,256]{2,0,1:T(8,128)(2,1)}), bf16[64,4,256]{2,0,1:T(8,128)(2,1)S(1)}, u32[]{:S(2)}, u32[]{:S(2)}) async-start(bf16[64,4,256]{2,0,1:T(8,128)(2,1)} %bitcast.328), calls=%async_computation.1 | async-start | bytes 262144 | tf_op jit(solution)/shard_map/all_to_all | solution.py:38
  9.2 3.3 %all-to-all-done.1 = bf16[64,4,256]{2,0,1:T(8,128)(2,1)S(1)} async-done(((bf16[64,4,256]{2,0,1:T(8,128)(2,1)}), bf16[64,4,256]{2,0,1:T(8,128)(2,1)S(1)}, u32[]{:S(2)}, u32[]{:S(2)}) %all-to-all-start.1) | async-done | bytes 131104 | tf_op jit(solution)/shard_map/all_to_all | solution.py:38
  12.5 3.3 %all-to-all-start.2 = ((bf16[64,4,256]{2,0,1:T(8,128)(2,1)}), bf16[64,4,256]{2,0,1:T(8,128)(2,1)S(1)}, u32[]{:S(2)}, u32[]{:S(2)}) async-start(bf16[64,4,256]{2,0,1:T(8,128)(2,1)} %bitcast.329), calls=%async_computation.2 | async-start | bytes 262144 | tf_op jit(solution)/shard_map/all_to_all | solution.py:39
  15.9 5.9 %all-to-all-done.2 = bf16[64,4,256]{2,0,1:T(8,128)(2,1)S(1)} async-done(((bf16[64,4,256]{2,0,1:T(8,128)(2,1)}), bf16[64,4,256]{2,0,1:T(8,128)(2,1)S(1)}, u32[]{:S(2)}, u32[]{:S(2)}) %all-to-all-start.2) | async-done | bytes 131104 | tf_op jit(solution)/shard_map/all_to_all | solution.py:39
  21.8 3.4 %all-to-all-start = ((bf16[64,4,512]{2,0,1:T(8,128)(2,1)}), bf16[64,4,512]{2,0,1:T(8,128)(2,1)S(1)}, u32[]{:S(2)}, u32[]{:S(2)}) async-start(bf16[64,4,512]{2,0,1:T(8,128)(2,1)} %bitcast.327), calls=%async_computation | async-start | bytes 524288 | tf_op jit(solution)/shard_map/all_to_all | solution.py:37
  27.4 4.8 %collective-permute-start.3 = (bf16[2,256,256]{2,1,0:T(8,128)(2,1)S(1)}, bf16[2,256,256]{2,1,0:T(8,128)(2,1)S(1)}, u32[]{:S(2)}, u32[]{:S(2)}) collective-permute-start(bf16[2,256,256]{2,1,0:T(8,128)(2,1)S(1)} %pad_maximum_fusion), channel_id=1, source_target_pairs={{0,16},{4,20},{8,24},{12,28},{16,32},{20,36},{24,40},{28,44},{32,4... | collective-permute-start | bytes 786440 | tf_op jit(solution)/shard_map/ppermute | solution.py:16
  32.2 1.9 %collective-permute-start.2 = (bf16[2,256,256]{2,1,0:T(8,128)(2,1)S(1)}, bf16[2,256,256]{2,1,0:T(8,128)(2,1)S(1)}, u32[]{:S(2)}, u32[]{:S(2)}) collective-permute-start(bf16[2,256,256]{2,1,0:T(8,128)(2,1)S(1)} %pad_maximum_fusion), channel_id=1, source_target_pairs={{0,12},{4,16},{8,20},{12,24},{16,28},{20,32},{24,36},{28,40},{32,4... | collective-permute-start | bytes 786440 | tf_op jit(solution)/shard_map/ppermute | solution.py:16
  34.1 3.5 %collective-permute-start.1 = (bf16[2,256,256]{2,1,0:T(8,128)(2,1)S(1)}, bf16[2,256,256]{2,1,0:T(8,128)(2,1)S(1)}, u32[]{:S(2)}, u32[]{:S(2)}) collective-permute-start(bf16[2,256,256]{2,1,0:T(8,128)(2,1)S(1)} %pad_maximum_fusion), channel_id=1, source_target_pairs={{0,8},{4,12},{8,16},{12,20},{16,24},{20,28},{24,32},{28,36},{32,40... | collective-permute-start | bytes 786440 | tf_op jit(solution)/shard_map/ppermute | solution.py:16
  37.6 4.3 %collective-permute-start = (bf16[2,256,256]{2,1,0:T(8,128)(2,1)S(1)}, bf16[2,256,256]{2,1,0:T(8,128)(2,1)S(1)}, u32[]{:S(2)}, u32[]{:S(2)}) collective-permute-start(bf16[2,256,256]{2,1,0:T(8,128)(2,1)S(1)} %pad_maximum_fusion), channel_id=1, source_target_pairs={{0,4},{4,8},{8,12},{12,16},{16,20},{20,24},{24,28},{28,32},{32,36}... | collective-permute-start | bytes 786440 | tf_op jit(solution)/shard_map/ppermute | solution.py:16
  42.7 4.7 %all-to-all-start.4 = ((bf16[64,4,512]{2,0,1:T(8,128)(2,1)}), bf16[64,4,512]{2,0,1:T(8,128)(2,1)S(1)}, u32[]{:S(2)}, u32[]{:S(2)}) async-start(bf16[64,4,512]{2,0,1:T(8,128)(2,1)} %bitcast.326), calls=%async_computation.4 | async-start | bytes 524288 | tf_op jit(solution)/shard_map/all_to_all | solution.py:40
  48.8 5.5 %all-to-all-done.4 = bf16[64,4,512]{2,0,1:T(8,128)(2,1)S(1)} async-done(((bf16[64,4,512]{2,0,1:T(8,128)(2,1)}), bf16[64,4,512]{2,0,1:T(8,128)(2,1)S(1)}, u32[]{:S(2)}, u32[]{:S(2)}) %all-to-all-start.4) | async-done | bytes 262176 | tf_op jit(solution)/shard_map/all_to_all | solution.py:40
  70.4 2.0 %fusion.60 = f32[2,2,256,128]{2,3,1,0:T(8,128)} fusion(bf16[256,2,128,1]{0,2,3,1:T(8,128)(2,1)} %bitcast.362, f32[2,2,256,256]{2,3,1,0:T(8,128)S(1)} %get-tuple-element.33, f32[2,2,256]{2,1,0:T(2,128)S(1)} %maximum_maximum_fusion), kind=kOutput, calls=%fused_computation.87 | convolution fusion | flops 67633152 | bytes 1708032 | tf_op jit(solution)/shard_map/xypq,qxa->xypa/dot_general | solution.py:80
  74.0 2.0 %fusion.58 = f32[2,2,256,128]{2,3,1,0:T(8,128)} fusion(bf16[256,2,128,1]{0,2,3,1:T(8,128)(2,1)} %bitcast.364, f32[2,2,256,256]{2,3,1,0:T(8,128)S(1)} %get-tuple-element.31, f32[2,2,256]{2,1,0:T(2,128)S(1)} %maximum_maximum_fusion), kind=kOutput, calls=%fused_computation.86 | convolution fusion | flops 67633152 | bytes 1708032 | tf_op jit(solution)/shard_map/xypq,qxa->xypa/dot_general | solution.py:80
  99.6 1.9 %collective-permute-start.5 = (bf16[2,256,256]{2,1,0:T(8,128)(2,1)}, bf16[2,256,256]{2,1,0:T(8,128)(2,1)}, u32[]{:S(2)}, u32[]{:S(2)}) collective-permute-start(bf16[2,256,256]{2,1,0:T(8,128)(2,1)} %pad_maximum_fusion.2), channel_id=1, source_target_pairs={{8,0},{12,4},{16,8},{20,12},{24,16},{28,20},{32,24},{36,28},{40,32... | collective-permute-start | bytes 786440 | tf_op jit(solution)/shard_map/ppermute | solution.py:16
  102.5 5.0 %collective-permute-start.6 = (bf16[2,256,256]{2,1,0:T(8,128)(2,1)}, bf16[2,256,256]{2,1,0:T(8,128)(2,1)}, u32[]{:S(2)}, u32[]{:S(2)}) collective-permute-start(bf16[2,256,256]{2,1,0:T(8,128)(2,1)} %pad_maximum_fusion.3), channel_id=1, source_target_pairs={{12,0},{16,4},{20,8},{24,12},{28,16},{32,20},{36,24},{40,28},{44,3... | collective-permute-start | bytes 786440 | tf_op jit(solution)/shard_map/ppermute | solution.py:16
  108.5 2.1 %collective-permute-start.7 = (bf16[2,256,256]{2,1,0:T(8,128)(2,1)}, bf16[2,256,256]{2,1,0:T(8,128)(2,1)}, u32[]{:S(2)}, u32[]{:S(2)}) collective-permute-start(bf16[2,256,256]{2,1,0:T(8,128)(2,1)} %pad_maximum_fusion.4), channel_id=1, source_target_pairs={{16,0},{20,4},{24,8},{28,12},{32,16},{36,20},{40,24},{44,28},{48,3... | collective-permute-start | bytes 786440 | tf_op jit(solution)/shard_map/ppermute | solution.py:16
  113.7 4.5 %all-to-all-start.5 = ((bf16[4,64,512]{2,1,0:T(8,128)(2,1)}), bf16[4,64,512]{2,1,0:T(8,128)(2,1)S(1)}, u32[]{:S(2)}, u32[]{:S(2)}) async-start(bf16[4,64,512]{2,1,0:T(8,128)(2,1)} %convert_element_type.105), calls=%async_computation.5 | async-start | bytes 524288 | tf_op jit(solution)/shard_map/all_to_all | solution.py:149
  119.2 3.7 %collective-permute-done.6 = bf16[2,256,256]{2,1,0:T(8,128)(2,1)} collective-permute-done((bf16[2,256,256]{2,1,0:T(8,128)(2,1)}, bf16[2,256,256]{2,1,0:T(8,128)(2,1)}, u32[]{:S(2)}, u32[]{:S(2)}) %collective-permute-start.6) | collective-permute-done | bytes 262176 | tf_op jit(solution)/shard_map/ppermute | solution.py:16
  122.9 11.8 %collective-permute-done.7 = bf16[2,256,256]{2,1,0:T(8,128)(2,1)} collective-permute-done((bf16[2,256,256]{2,1,0:T(8,128)(2,1)}, bf16[2,256,256]{2,1,0:T(8,128)(2,1)}, u32[]{:S(2)}, u32[]{:S(2)}) %collective-permute-start.7) | collective-permute-done | bytes 262176 | tf_op jit(solution)/shard_map/ppermute | solution.py:16
  136.0 3.9 %all-to-all-start.3 = ((bf16[4,64,512]{2,1,0:T(8,128)(2,1)}), bf16[4,64,512]{2,1,0:T(8,128)(2,1)S(1)}, u32[]{:S(2)}, u32[]{:S(2)}) async-start(bf16[4,64,512]{2,1,0:T(8,128)(2,1)} %all_to_all.107), calls=%async_computation.3 | async-start | bytes 524288 | tf_op jit(solution)/shard_map/all_to_all | solution.py:148
  140.6 6.0 %all-to-all-done.3 = bf16[4,64,512]{2,1,0:T(8,128)(2,1)S(1)} async-done(((bf16[4,64,512]{2,1,0:T(8,128)(2,1)}), bf16[4,64,512]{2,1,0:T(8,128)(2,1)S(1)}, u32[]{:S(2)}, u32[]{:S(2)}) %all-to-all-start.3) | async-done | bytes 262176 | tf_op jit(solution)/shard_map/all_to_all | solution.py:148
  146.6 8.3 %all_to_all.131 = bf16[4,64,256]{2,1,0:T(8,128)(2,1)S(1)} all-to-all(bf16[4,64,256]{2,1,0:T(8,128)(2,1)S(1)} %bitcast.359), channel_id=1, replica_groups=mesh['pipe'=192,'tensor'=4] {'tensor'}, dimensions={0} | all-to-all | bytes 262144 | tf_op jit(solution)/shard_map/all_to_all | solution.py:150
  155.0 3.3 %all-to-all-start.7 = ((bf16[4,64,256]{2,1,0:T(8,128)(2,1)}), bf16[4,64,256]{2,1,0:T(8,128)(2,1)S(1)}, u32[]{:S(2)}, u32[]{:S(2)}) async-start(bf16[4,64,256]{2,1,0:T(8,128)(2,1)} %bitcast.115), calls=%async_computation.7 | async-start | bytes 262144 | tf_op jit(solution)/shard_map/all_to_all | solution.py:151
  160.4 3.8 %all-to-all-done.7 = bf16[4,64,256]{2,1,0:T(8,128)(2,1)S(1)} async-done(((bf16[4,64,256]{2,1,0:T(8,128)(2,1)}), bf16[4,64,256]{2,1,0:T(8,128)(2,1)S(1)}, u32[]{:S(2)}, u32[]{:S(2)}) %all-to-all-start.7) | async-done | bytes 131104 | tf_op jit(solution)/shard_map/all_to_all | solution.py:151
  (164 shorter events, 60.1 us)
Async XLA Ops:
  0.6 5.9 %copy-start.25 = (bf16[64,2048]{1,0:T(8,128)(2,1)S(1)}, bf16[64,2048]{1,0:T(8,128)(2,1)}, u32[]{:S(2)}) copy-start(bf16[64,2048]{1,0:T(8,128)(2,1)} %param.5) | copy-start | bytes 786436
  2.3 10.3 %all-to-all-start.1 = ((bf16[64,4,256]{2,0,1:T(8,128)(2,1)}), bf16[64,4,256]{2,0,1:T(8,128)(2,1)S(1)}, u32[]{:S(2)}, u32[]{:S(2)}) async-start(bf16[64,4,256]{2,0,1:T(8,128)(2,1)} %bitcast.328), calls=%async_computation.1 | async-start | bytes 262144 | tf_op jit(solution)/shard_map/all_to_all | solution.py:38
  12.5 9.3 %all-to-all-start.2 = ((bf16[64,4,256]{2,0,1:T(8,128)(2,1)}), bf16[64,4,256]{2,0,1:T(8,128)(2,1)S(1)}, u32[]{:S(2)}, u32[]{:S(2)}) async-start(bf16[64,4,256]{2,0,1:T(8,128)(2,1)} %bitcast.329), calls=%async_computation.2 | async-start | bytes 262144 | tf_op jit(solution)/shard_map/all_to_all | solution.py:39
  21.8 20.9 %all-to-all-start = ((bf16[64,4,512]{2,0,1:T(8,128)(2,1)}), bf16[64,4,512]{2,0,1:T(8,128)(2,1)S(1)}, u32[]{:S(2)}, u32[]{:S(2)}) async-start(bf16[64,4,512]{2,0,1:T(8,128)(2,1)} %bitcast.327), calls=%async_computation | async-start | bytes 524288 | tf_op jit(solution)/shard_map/all_to_all | solution.py:37
  27.4 27.8 %collective-permute-start.3 = (bf16[2,256,256]{2,1,0:T(8,128)(2,1)S(1)}, bf16[2,256,256]{2,1,0:T(8,128)(2,1)S(1)}, u32[]{:S(2)}, u32[]{:S(2)}) collective-permute-start(bf16[2,256,256]{2,1,0:T(8,128)(2,1)S(1)} %pad_maximum_fusion), channel_id=1, source_target_pairs={{0,16},{4,20},{8,24},{12,28},{16,32},{20,36},{24,40},{28,44},{32,4... | collective-permute-start | bytes 786440 | tf_op jit(solution)/shard_map/ppermute | solution.py:16
  32.2 23.7 %collective-permute-start.2 = (bf16[2,256,256]{2,1,0:T(8,128)(2,1)S(1)}, bf16[2,256,256]{2,1,0:T(8,128)(2,1)S(1)}, u32[]{:S(2)}, u32[]{:S(2)}) collective-permute-start(bf16[2,256,256]{2,1,0:T(8,128)(2,1)S(1)} %pad_maximum_fusion), channel_id=1, source_target_pairs={{0,12},{4,16},{8,20},{12,24},{16,28},{20,32},{24,36},{28,40},{32,4... | collective-permute-start | bytes 786440 | tf_op jit(solution)/shard_map/ppermute | solution.py:16
  34.1 23.5 %collective-permute-start.1 = (bf16[2,256,256]{2,1,0:T(8,128)(2,1)S(1)}, bf16[2,256,256]{2,1,0:T(8,128)(2,1)S(1)}, u32[]{:S(2)}, u32[]{:S(2)}) collective-permute-start(bf16[2,256,256]{2,1,0:T(8,128)(2,1)S(1)} %pad_maximum_fusion), channel_id=1, source_target_pairs={{0,8},{4,12},{8,16},{12,20},{16,24},{20,28},{24,32},{28,36},{32,40... | collective-permute-start | bytes 786440 | tf_op jit(solution)/shard_map/ppermute | solution.py:16
  37.6 21.0 %collective-permute-start = (bf16[2,256,256]{2,1,0:T(8,128)(2,1)S(1)}, bf16[2,256,256]{2,1,0:T(8,128)(2,1)S(1)}, u32[]{:S(2)}, u32[]{:S(2)}) collective-permute-start(bf16[2,256,256]{2,1,0:T(8,128)(2,1)S(1)} %pad_maximum_fusion), channel_id=1, source_target_pairs={{0,4},{4,8},{8,12},{12,16},{16,20},{20,24},{24,28},{28,32},{32,36}... | collective-permute-start | bytes 786440 | tf_op jit(solution)/shard_map/ppermute | solution.py:16
  42.0 5.5 %copy-start.18 = (bf16[256,2,128]{2,1,0:T(2,128)(2,1)}, bf16[256,2,128]{2,1,0:T(2,128)(2,1)S(1)}, u32[]{:S(2)}) copy-start(bf16[256,2,128]{2,1,0:T(2,128)(2,1)S(1)} %reshape_squeeze_stack.8) | copy-start | bytes 393220
  42.7 11.5 %all-to-all-start.4 = ((bf16[64,4,512]{2,0,1:T(8,128)(2,1)}), bf16[64,4,512]{2,0,1:T(8,128)(2,1)S(1)}, u32[]{:S(2)}, u32[]{:S(2)}) async-start(bf16[64,4,512]{2,0,1:T(8,128)(2,1)} %bitcast.326), calls=%async_computation.4 | async-start | bytes 524288 | tf_op jit(solution)/shard_map/all_to_all | solution.py:40
  56.6 3.5 %copy-start.8 = (bf16[1,256,256]{1,2,0:T(8,128)(2,1)}, bf16[1,256,256]{1,2,0:T(8,128)(2,1)S(1)}, u32[]{:S(2)}) copy-start(bf16[1,256,256]{1,2,0:T(8,128)(2,1)S(1)} %copy.212) | copy-start | bytes 393220
  56.8 3.7 %copy-start.10 = (bf16[1,256,256]{1,2,0:T(8,128)(2,1)}, bf16[1,256,256]{1,2,0:T(8,128)(2,1)S(1)}, u32[]{:S(2)}) copy-start(bf16[1,256,256]{1,2,0:T(8,128)(2,1)S(1)} %copy.210) | copy-start | bytes 393220
  93.9 4.5 %copy-start.4 = (bf16[2,2,256,256]{2,3,1,0:T(8,128)(2,1)S(1)}, bf16[2,2,256,256]{2,3,1,0:T(8,128)(2,1)}, u32[]{:S(2)}) copy-start(bf16[2,2,256,256]{2,3,1,0:T(8,128)(2,1)} %fusion.19) | copy-start | bytes 1572868
  94.7 3.6 %copy-start.31 = (bf16[2,256,128]{1,2,0:T(8,128)(2,1)S(1)}, bf16[2,256,128]{1,2,0:T(8,128)(2,1)}, u32[]{:S(2)}) copy-start(bf16[2,256,128]{1,2,0:T(8,128)(2,1)} %fusion.40) | copy-start | bytes 393220
  96.4 22.8 %collective-permute-start.4 = (bf16[2,256,256]{2,1,0:T(8,128)(2,1)}, bf16[2,256,256]{2,1,0:T(8,128)(2,1)}, u32[]{:S(2)}, u32[]{:S(2)}) collective-permute-start(bf16[2,256,256]{2,1,0:T(8,128)(2,1)} %pad_maximum_fusion.1), channel_id=1, source_target_pairs={{4,0},{8,4},{12,8},{16,12},{20,16},{24,20},{28,24},{32,28},{36,32}... | collective-permute-start | bytes 786440 | tf_op jit(solution)/shard_map/ppermute | solution.py:16
  99.6 19.6 %collective-permute-start.5 = (bf16[2,256,256]{2,1,0:T(8,128)(2,1)}, bf16[2,256,256]{2,1,0:T(8,128)(2,1)}, u32[]{:S(2)}, u32[]{:S(2)}) collective-permute-start(bf16[2,256,256]{2,1,0:T(8,128)(2,1)} %pad_maximum_fusion.2), channel_id=1, source_target_pairs={{8,0},{12,4},{16,8},{20,12},{24,16},{28,20},{32,24},{36,28},{40,32... | collective-permute-start | bytes 786440 | tf_op jit(solution)/shard_map/ppermute | solution.py:16
  101.8 5.8 %copy-start.33 = (bf16[2,256,128]{1,2,0:T(8,128)(2,1)S(1)}, bf16[2,256,128]{1,2,0:T(8,128)(2,1)}, u32[]{:S(2)}) copy-start(bf16[2,256,128]{1,2,0:T(8,128)(2,1)} %fusion.42) | copy-start | bytes 393220
  102.5 20.4 %collective-permute-start.6 = (bf16[2,256,256]{2,1,0:T(8,128)(2,1)}, bf16[2,256,256]{2,1,0:T(8,128)(2,1)}, u32[]{:S(2)}, u32[]{:S(2)}) collective-permute-start(bf16[2,256,256]{2,1,0:T(8,128)(2,1)} %pad_maximum_fusion.3), channel_id=1, source_target_pairs={{12,0},{16,4},{20,8},{24,12},{28,16},{32,20},{36,24},{40,28},{44,3... | collective-permute-start | bytes 786440 | tf_op jit(solution)/shard_map/ppermute | solution.py:16
  107.8 2.8 %copy-start.27 = (f32[2,256,128,1]{1,2,3,0:T(8,128)S(1)}, f32[2,256,128,1]{1,2,3,0:T(8,128)}, u32[]{:S(2)}) copy-start(f32[2,256,128,1]{1,2,3,0:T(8,128)} %fusion.75) | copy-start | bytes 786436
  108.5 26.1 %collective-permute-start.7 = (bf16[2,256,256]{2,1,0:T(8,128)(2,1)}, bf16[2,256,256]{2,1,0:T(8,128)(2,1)}, u32[]{:S(2)}, u32[]{:S(2)}) collective-permute-start(bf16[2,256,256]{2,1,0:T(8,128)(2,1)} %pad_maximum_fusion.4), channel_id=1, source_target_pairs={{16,0},{20,4},{24,8},{28,12},{32,16},{36,20},{40,24},{44,28},{48,3... | collective-permute-start | bytes 786440 | tf_op jit(solution)/shard_map/ppermute | solution.py:16
  113.7 4.5 %copy-start.16 = (bf16[256,2,2,128]{0,3,2,1:T(8,128)(2,1)S(1)}, bf16[256,2,2,128]{0,3,2,1:T(8,128)(2,1)}, u32[]{:S(2)}) copy-start(bf16[256,2,2,128]{0,3,2,1:T(8,128)(2,1)} %get-tuple-element.40) | copy-start | bytes 786436
  113.7 22.3 %all-to-all-start.5 = ((bf16[4,64,512]{2,1,0:T(8,128)(2,1)}), bf16[4,64,512]{2,1,0:T(8,128)(2,1)S(1)}, u32[]{:S(2)}, u32[]{:S(2)}) async-start(bf16[4,64,512]{2,1,0:T(8,128)(2,1)} %convert_element_type.105), calls=%async_computation.5 | async-start | bytes 524288 | tf_op jit(solution)/shard_map/all_to_all | solution.py:149
  136.0 10.6 %all-to-all-start.3 = ((bf16[4,64,512]{2,1,0:T(8,128)(2,1)}), bf16[4,64,512]{2,1,0:T(8,128)(2,1)S(1)}, u32[]{:S(2)}, u32[]{:S(2)}) async-start(bf16[4,64,512]{2,1,0:T(8,128)(2,1)} %all_to_all.107), calls=%async_computation.3 | async-start | bytes 524288 | tf_op jit(solution)/shard_map/all_to_all | solution.py:148
  155.0 9.3 %all-to-all-start.7 = ((bf16[4,64,256]{2,1,0:T(8,128)(2,1)}), bf16[4,64,256]{2,1,0:T(8,128)(2,1)S(1)}, u32[]{:S(2)}, u32[]{:S(2)}) async-start(bf16[4,64,256]{2,1,0:T(8,128)(2,1)} %bitcast.115), calls=%async_computation.7 | async-start | bytes 262144 | tf_op jit(solution)/shard_map/all_to_all | solution.py:151
  (26 other events, 31.2 us)
where the time goes:
time: 166 us; the launch traced here: 165 us
  starting transfers between devices  53 us (32%)
  waiting for transfers between devices  41.2 us (25%)
  local copies, waits for them, and re-layouts  29.4 us (18%)
  matrix products  23.2 us (14%)
  other arithmetic  8.54 us (5%)
  blocking collectives  8.35 us (5%)
    ppermute x8, starting transfers between devices, shifted(): lax.ppermute(value, axis, [(source, source + steps) for source in range(i...  25.5 us
    ppermute x8, waiting for transfers between devices, shifted(): lax.ppermute(value, axis, [(source, source + steps) for source in range(i...  16.6 us
    slice x7, local copies, waits for them, and re-layouts, body(): weighted_value_tensor = tiles[lag][1].reshape(tok, kv_local, HEAD_DIM)  8.65 us
    all_to_all x1, blocking collectives, body(): lax.all_to_all(grad_k_rows, 'tensor', split_axis=0, concat_axis=1, tiled=...  8.35 us
    dot_general x5, matrix products, body(): jnp.einsum('xypq,qxa->xypa', expos[lag].astype(jnp.bfloat16), weighted_va...  8.02 us
    all_to_all x1, waiting for transfers between devices, body(): lax.all_to_all(out_rows, 'tensor', split_axis=0, concat_axis=1, tiled=True)  6.02 us
    all_to_all x1, waiting for transfers between devices, body(): lax.all_to_all(value, 'tensor', split_axis=1, concat_axis=0, tiled=True)  5.93 us
    all_to_all x1, waiting for transfers between devices, body(): lax.all_to_all(grad_out, 'tensor', split_axis=1, concat_axis=0, tiled=True)  5.46 us
  transfers between devices with their start and end apart: 15, of which 9 were waited for; matrix products, arithmetic and copies ran while one was open for 12% of the time, Pallas kernels for 0%

commit v1 on v0

v1 whole, which is shorter than its diff:
```python
import functools
import math

import jax
import jax.numpy as jnp
from jax import lax
from jax.experimental import pallas as pl
from jax.experimental.pallas import tpu as pltpu
from jax.sharding import PartitionSpec as P

MESH = pl.DeviceIdType.MESH
D = 128
WINDOW = 1024
SCALE = 168.0 ** -0.5
C2 = SCALE * math.log2(math.e)
NEG = -1e30
F32 = jnp.float32
BF16 = jnp.bfloat16
B = 256
PIECE = 64
TILES = 5
ORDER = ((2, 0), (2, 1), (1, 0), (1, 1), (3, 0), (3, 1), (0, 1))
ARRIVE = ((0, 0), (0, 1), (1, 0), (3, 0), (1, 1), (3, 1), (2, 0), (2, 1))


def dot_nt(a, b):
    return lax.dot_general(a, b, (((1,), (1,)), ((), ())), preferred_element_type=F32)


def dot_nn(a, b):
    return jnp.dot(a, b, preferred_element_type=F32)


def wide(x):
    return jnp.concatenate([x, x], axis=1)


def kernel(pipe, q_ref, k_ref, v_ref, g_ref, seg_ref, o_out, dq_out, dk_out, dv_out,
           qst, gst, kbuf, vbuf, bias, pbuf, mtile, mrun, lrun, acc, delta,
           qT, gT, dkT, dvT, obuf, dqbuf, snd2, rcv2, snd1, rcv1, fin,
           in_send, in_recv, own_sem, halo_send, halo_recv, ret_send, ret_recv,
           out_send, out_recv, out_own):
    p = lax.axis_index("pipe")
    t = lax.axis_index("tensor")
    core = p % 2
    chip = p // 2
    nxt = ((p + 2) % pipe, t)
    prv = ((p + pipe - 2) % pipe, t)
    head = 2 * t + core

    def peer(dx, dc):
        c = (core + dc) % 2
        return c, (t + dx) % 4

    def source(dx, dc):
        c = (core + dc) % 2
        return c, (t + 4 - dx) % 4

    barrier = pltpu.get_barrier_semaphore()
    for dx, dc in ORDER:
        c, x = peer(dx, dc)
        pl.semaphore_signal(barrier, inc=1, device_id=(chip * 2 + c, x), device_id_type=MESH)
    pl.semaphore_signal(barrier, inc=1, device_id=nxt, device_id_type=MESH)
    pl.semaphore_signal(barrier, inc=1, device_id=prv, device_id_type=MESH)
    pl.semaphore_wait(barrier, 9)

    def src_of(a, head_of):
        if a == 0:
            return k_ref.at[:, pl.ds(pl.multiple_of(head_of * D, D), D)]
        if a == 1:
            return v_ref.at[:, pl.ds(pl.multiple_of(head_of * D, D), D)]
        h = a % 2
        ref = q_ref if a < 4 else g_ref
        return ref.at[:, pl.ds(pl.multiple_of((2 * head_of + h) * D, D), D)]

    def dst_of(a, c, x):
        if a < 2:
            ref = kbuf if a == 0 else vbuf
            return ref.at[pl.ds(pl.multiple_of(4 * B + c * B + x * PIECE, PIECE), PIECE), :]
        h = a % 2
        ref = qst if a < 4 else gst
        return ref.at[c, pl.ds(pl.multiple_of(h * B + x * PIECE, PIECE), PIECE), :]

    def exchange(a, dx, dc, landing):
        c, x = peer(dx, dc)
        sc, sx = source(dx, dc) if landing else (core, t)
        return pltpu.make_async_remote_copy(
            src_ref=src_of(a, 2 * x + c), dst_ref=dst_of(a, sc, sx),
            send_sem=in_send.at[a, dx, dc], recv_sem=in_recv.at[a, dx, dc],
            device_id=(chip * 2 + c, x), device_id_type=MESH)

    def own(a):
        return pltpu.make_async_copy(src_of(a, head), dst_of(a, core, t), own_sem.at[a])

    def rows_at(ref, block, c, x):
        return ref.at[pl.ds(pl.multiple_of(block * 2 * B + c * B + x * PIECE, PIECE), PIECE), :]

    def halo(hop, a, dx, dc):
        c, x = source(dx, dc)
        ref = kbuf if a == 0 else vbuf
        if hop == 0 and (dx, dc) == (0, 0):
            src = src_of(a, head)
        else:
            src = rows_at(ref, 2 - hop, c, x)
        return pltpu.make_async_remote_copy(
            src_ref=src, dst_ref=rows_at(ref, 1 - hop, c, x),
            send_sem=halo_send.at[hop, a, dx, dc], recv_sem=halo_recv.at[hop, a, dx, dc],
            device_id=nxt, device_id_type=MESH)

    for a in range(6):
        for dx, dc in ORDER:
            exchange(a, dx, dc, False).start()
        own(a).start()
        if a < 2:
            halo(0, a, 0, 0).start()

    row = lax.broadcasted_iota(jnp.int32, (B, D), 0)
    col = lax.broadcasted_iota(jnp.int32, (B, D), 1)

    def seg_row(r):
        at = chip * 4 - 8 + r
        s = seg_ref[pl.ds(jnp.maximum(at, 0), 1), :]
        return jnp.where(at >= 0, s, -1)

    for b in range(2):
        qcols = []
        for part in range(2):
            s = jnp.broadcast_to(seg_row(8 + 2 * b + part), (D, D))
            qcols.append(jnp.transpose(s))
        qseg = jnp.concatenate(qcols, axis=0)

        def mask_tile(l, carry):
            i = b + l
            for part in range(2):
                kseg = jnp.broadcast_to(seg_row(2 * i + part), (B, D))
                gap = row - col + (b * B + 4 * B - i * B - part * D)
                ok = (kseg == qseg) & (gap >= 0) & (gap < WINDOW)
                bias[b, l, :, part * D:(part + 1) * D] = jnp.where(ok, 0.0, NEG)
            return carry

        lax.fori_loop(0, TILES, mask_tile, 0)

    mrun[...] = jnp.full(mrun.shape, NEG, F32)
    lrun[...] = jnp.zeros(lrun.shape, F32)
    acc[...] = jnp.zeros(acc.shape, F32)

    for a in range(2):
        own(a).wait()
        for dx, dc in ARRIVE[1:]:
            exchange(a, dx, dc, True).wait_recv()
            halo(0, a, dx, dc).start()

    def pass_on(a):
        for dx, dc in ARRIVE:
            halo(0, a, dx, dc).wait_recv()
            halo(1, a, dx, dc).start()

    def arrived(a):
        own(a).wait()
        for dx, dc in ARRIVE[1:]:
            exchange(a, dx, dc, True).wait_recv()

    def k_tile(i):
        return kbuf[pl.ds(pl.multiple_of(i * B, B), B), :]

    def v_tile(i):
        return vbuf[pl.ds(pl.multiple_of(i * B, B), B), :]

    def forward(b, i):
        l = i - b
        n = b * TILES + l
        s = dot_nt(qst[b], k_tile(i)) * C2
        bias_t = bias[b, l]
        s = s + jnp.concatenate([bias_t, bias_t], axis=0)
        m_old = mrun[b]
        m_new = jnp.maximum(m_old, jnp.max(s, axis=1, keepdims=True))
        e = jnp.exp2(s - wide(m_new))
        alpha = jnp.exp2(m_old - m_new)
        mrun[b] = m_new
        mtile[n] = m_new
        lrun[b] = lrun[b] * alpha + jnp.sum(e, axis=1, keepdims=True)
        e16 = e.astype(BF16)
        pbuf[n] = e16
        acc[b] = acc[b] * alpha + dot_nn(e16, v_tile(i))

    pass_on(0)
    for a in (2, 3):
        arrived(a)

    def phase1(n, carry):
        forward(jnp.minimum(n, 1), 4 + n % 2)
        return carry

    lax.fori_loop(0, 3, phase1, 0)
    pass_on(1)

    def phase2(n, carry):
        forward(n // 2, 3 - n % 2)
        return carry

    lax.fori_loop(0, 4, phase2, 0)
    for a in (4, 5):
        arrived(a)
    for b in range(2):
        qT[b] = jnp.transpose(qst[b].astype(F32)).astype(BF16)
        gT[b] = jnp.transpose(gst[b].astype(F32)).astype(BF16)
    dkT[...] = jnp.zeros(dkT.shape, F32)
    dvT[...] = jnp.zeros(dvT.shape, F32)
    for a in range(2):
        for dx, dc in ARRIVE:
            halo(1, a, dx, dc).wait_recv()

    def phase3(n, carry):
        forward(n // 2, 1 - n % 2)
        return carry

    lax.fori_loop(0, 3, phase3, 0)

    def out_src(a, c, x):
        if a < 4:
            ref = obuf if a < 2 else dqbuf
            return ref.at[c, pl.ds(pl.multiple_of((a % 2) * B + x * PIECE, PIECE), PIECE), :]
        return fin.at[a - 4, c, pl.ds(pl.multiple_of(x * PIECE, PIECE), PIECE), :]

    def out_dst(a, head_of):
        if a < 4:
            ref = o_out if a < 2 else dq_out
            return ref.at[:, pl.ds(pl.multiple_of((2 * head_of + a % 2) * D, D), D)]
        ref = dk_out if a == 4 else dv_out
        return ref.at[:, pl.ds(pl.multiple_of(head_of * D, D), D)]

    def give(a, dx, dc, landing):
        c, x = peer(dx, dc)
        if landing:
            sc, sx = source(dx, dc)
            from_head = 2 * sx + sc
        else:
            from_head = head
        return pltpu.make_async_remote_copy(
            src_ref=out_src(a, c, x), dst_ref=out_dst(a, from_head),
            send_sem=out_send.at[a, dx, dc], recv_sem=out_recv.at[a, dx, dc],
            device_id=(chip * 2 + c, x), device_id_type=MESH)

    def keep(a):
        return pltpu.make_async_copy(out_src(a, core, t), out_dst(a, head), out_own.at[a])

    def give_all(a):
        for dx, dc in ORDER:
            give(a, dx, dc, False).start()
        keep(a).start()

    for b in range(2):
        linv = 1.0 / lrun[b]
        lrun[b] = linv
        o16 = (acc[b] * linv).astype(BF16)
        obuf[b] = o16
        d = jnp.sum(gst[b].astype(F32) * o16.astype(F32), axis=1, keepdims=True)
        delta[b] = jnp.broadcast_to(d, (2 * B, D))
    acc[...] = jnp.zeros(acc.shape, F32)

    def backward(b, i):
        n = b * TILES + i - b
        r = jnp.exp2(mtile[n] - mrun[b]) * lrun[b]
        prob = pbuf[n].astype(F32) * wide(r)
        dp = dot_nt(gst[b], v_tile(i))
        ds = (prob * (dp - wide(delta[b]))).astype(BF16)
        dvT[i] += dot_nn(gT[b], prob.astype(BF16))
        dkT[i] += dot_nn(qT[b], ds)
        acc[b] += dot_nn(ds, k_tile(i))

    def back(hop, i, a):
        s, r = (snd2, rcv2) if hop == 0 else (snd1, rcv1)
        return pltpu.make_async_remote_copy(
            src_ref=s.at[i, a], dst_ref=r.at[i, a],
            send_sem=ret_send.at[hop, i, a], recv_sem=ret_recv.at[hop, i, a],
            device_id=prv, device_id_type=MESH)

    def phase4(n, carry):
        backward(n // 2, (n + 1) // 2)
        return carry

    backward(0, 0)
    for a, ref in ((0, dkT), (1, dvT)):
        snd2[0, a] = ref[0].astype(BF16)
        back(0, 0, a).start()
    for a in range(2):
        give_all(a)

    def pair(n, carry):
        backward(n % 2, 1 + n // 2)
        return carry

    lax.fori_loop(0, 2, pair, 0)
    for a, ref in ((0, dkT), (1, dvT)):
        snd2[1, a] = ref[1].astype(BF16)
        back(0, 1, a).start()
    lax.fori_loop(2, 6, pair, 0)
    for i in range(2):
        for a, ref in ((0, dkT), (1, dvT)):
            back(0, i, a).wait_recv()
            snd1[i, a] = (ref[2 + i] + rcv2[i, a].astype(F32)).astype(BF16)
            back(1, i, a).start()
    lax.fori_loop(6, 8, pair, 0)
    backward(1, 5)
    for b in range(2):
        dqbuf[b] = (acc[b] * SCALE).astype(BF16)
    for a in (2, 3):
        give_all(a)
    for i in range(2):
        for a, ref in ((0, dkT), (1, dvT)):
            back(1, i, a).wait_recv()
            total = ref[4 + i] + rcv1[i, a].astype(F32)
            if a == 0:
                total = total * SCALE
            fin[a, i] = jnp.transpose(total).astype(BF16)
    for a in (4, 5):
        give_all(a)

    for a in range(6):
        for dx, dc in ORDER:
            exchange(a, dx, dc, False).wait_send()
            give(a, dx, dc, False).wait_send()
            give(a, dx, dc, True).wait_recv()
        keep(a).wait()
    for hop in range(2):
        for a in range(2):
            for dx, dc in ARRIVE:
                halo(hop, a, dx, dc).wait_send()
            for i in range(2):
                back(hop, i, a).wait_send()


def body(pipe, query, key, value, grad_out, segment_ids):
    seg = segment_ids.reshape(-1, D)
    anyspace = pl.BlockSpec(memory_space=pl.ANY)
    dma = pltpu.SemaphoreType.DMA
    return pl.pallas_call(
        functools.partial(kernel, pipe),
        out_shape=tuple(jax.ShapeDtypeStruct(x.shape, BF16) for x in (query, query, key, value)),
        in_specs=[anyspace] * 4 + [pl.BlockSpec(memory_space=pltpu.VMEM)],
        out_specs=(anyspace,) * 4,
        scratch_shapes=[
            pltpu.VMEM((2, 2 * B, D), BF16),
            pltpu.VMEM((2, 2 * B, D), BF16),
            pltpu.VMEM((6 * B, D), BF16),
            pltpu.VMEM((6 * B, D), BF16),
            pltpu.VMEM((2, TILES, B, B), F32),
            pltpu.VMEM((2 * TILES, 2 * B, B), BF16),
            pltpu.VMEM((2 * TILES, 2 * B, D), F32),
            pltpu.VMEM((2, 2 * B, D), F32),
            pltpu.VMEM((2, 2 * B, D), F32),
            pltpu.VMEM((2, 2 * B, D), F32),
            pltpu.VMEM((2, 2 * B, D), F32),
            pltpu.VMEM((2, D, 2 * B), BF16),
            pltpu.VMEM((2, D, 2 * B), BF16),
            pltpu.VMEM((6, D, B), F32),
            pltpu.VMEM((6, D, B), F32),
            pltpu.VMEM((2, 2 * B, D), BF16),
            pltpu.VMEM((2, 2 * B, D), BF16),
            pltpu.VMEM((2, 2, D, B), BF16),
            pltpu.VMEM((2, 2, D, B), BF16),
            pltpu.VMEM((2, 2, D, B), BF16),
            pltpu.VMEM((2, 2, D, B), BF16),
            pltpu.VMEM((2, 2, B, D), BF16),
            dma((6, 4, 2)), dma((6, 4, 2)), dma((6,)),
            dma((2, 2, 4, 2)), dma((2, 2, 4, 2)),
            dma((2, 2, 2)), dma((2, 2, 2)),
            dma((6, 4, 2)), dma((6, 4, 2)), dma((6,)),
        ],
        compiler_params=pltpu.CompilerParams(
            collective_id=0, has_side_effects=True, vmem_limit_bytes=40 * 1024 * 1024),
    )(query, key, value, grad_out, seg)


def solution(mesh):
    spec = P(("pipe", "tensor"), None)
    return jax.shard_map(
        functools.partial(body, mesh.shape["pipe"]),
        mesh=mesh,
        in_specs=(spec,) * 4 + (P(),),
        out_specs=(spec,) * 4,
        check_vma=False,
    )
```

time: 166 us -> 64.1 us (0.39)
  the two profiles are of different devices: /device:TPU:240 before, /device:TPU:1 now
where the time goes in v1:
time: 64.1 us; the launch traced here: 63.8 us
  Pallas kernels  55.8 us (87%)
  local copies, waits for them, and re-layouts  7.34 us (11%)
  between operations  0.65 us (1%)
    pallas_call x1, Pallas kernels, body(): pl.pallas_call(functools.partial(kernel, pipe), out_shape=tuple((jax.Shap...  55.8 us
    unnamed x14, local copies, waits for them, and re-layouts  7.34 us

profile of v1, /device:TPU:1, one launch (start us, length us, event | category | flops | bytes accessed | tf_op | source)
XLA Modules:
  0.0 63.8 jit_solution(9714018367476605786)
XLA Ops:
  0.6 0.0 copy-start
  0.6 0.9 %copy-done = bf16[64,2048]{1,0:T(8,128)(2,1)S(1)} copy-done((bf16[64,2048]{1,0:T(8,128)(2,1)S(1)}, bf16[64,2048]{1,0:T(8,128)(2,1)}, u32[]{:S(2)}) %copy-start) | copy-done | bytes 262168
  1.6 0.0 copy-start.1
  1.6 0.9 %copy-done.1 = bf16[64,2048]{1,0:T(8,128)(2,1)S(1)} copy-done((bf16[64,2048]{1,0:T(8,128)(2,1)S(1)}, bf16[64,2048]{1,0:T(8,128)(2,1)}, u32[]{:S(2)}) %copy-start.1) | copy-done | bytes 262168
  2.5 0.0 copy-start.2
  2.5 0.9 %copy-done.2 = s32[49152]{0:T(1024)S(1)} copy-done((s32[49152]{0:T(1024)S(1)}, s32[49152]{0:T(1024)}, u32[]{:S(2)}) %copy-start.2) | copy-done | bytes 196632
  3.5 0.0 copy-start.3
  3.5 0.9 %copy-done.3 = bf16[64,1024]{1,0:T(8,128)(2,1)S(1)} copy-done((bf16[64,1024]{1,0:T(8,128)(2,1)S(1)}, bf16[64,1024]{1,0:T(8,128)(2,1)}, u32[]{:S(2)}) %copy-start.3) | copy-done | bytes 131096
  4.4 0.0 copy-start.4
  4.4 0.9 %copy-done.4 = bf16[64,1024]{1,0:T(8,128)(2,1)S(1)} copy-done((bf16[64,1024]{1,0:T(8,128)(2,1)S(1)}, bf16[64,1024]{1,0:T(8,128)(2,1)}, u32[]{:S(2)}) %copy-start.4) | copy-done | bytes 131096
  5.3 55.8 %shard_map.84 = (bf16[64,2048]{1,0:T(8,128)(2,1)S(1)}, bf16[64,2048]{1,0:T(8,128)(2,1)S(1)}, bf16[64,1024]{1,0:T(8,128)(2,1)S(1)}, bf16[64,1024]{1,0:T(8,128)(2,1)S(1)}) custom-call(bf16[64,2048]{1,0:T(8,128)(2,1)S(1)} %copy-done, bf16[64,1024]{1,0:T(8,128)(2,1)S(1)} %copy-done.3, bf16[64,1024]{1,0:T(8,128)(2,1)S(1)} %copy-done.4, ...), custom_call_target="tpu_custom_call" | custom-call | tf_op jit(solution)/shard_map/pallas_call | solution.py:337
  61.1 0.7 %copy.13 = bf16[64,2048]{1,0:T(8,128)(2,1)} copy(bf16[64,2048]{1,0:T(8,128)(2,1)S(1)} %get-tuple-element.8) | data formatting | bytes 524288
  61.8 0.7 %copy.14 = bf16[64,2048]{1,0:T(8,128)(2,1)} copy(bf16[64,2048]{1,0:T(8,128)(2,1)S(1)} %get-tuple-element.9) | data formatting | bytes 524288
  62.5 0.7 %copy.15 = bf16[64,1024]{1,0:T(8,128)(2,1)} copy(bf16[64,1024]{1,0:T(8,128)(2,1)S(1)} %get-tuple-element.10) | data formatting | bytes 262144
  63.1 0.7 %copy.16 = bf16[64,1024]{1,0:T(8,128)(2,1)} copy(bf16[64,1024]{1,0:T(8,128)(2,1)S(1)} %get-tuple-element.11) | data formatting | bytes 262144
Async XLA Ops:
  0.6 1.0 %copy-start = (bf16[64,2048]{1,0:T(8,128)(2,1)S(1)}, bf16[64,2048]{1,0:T(8,128)(2,1)}, u32[]{:S(2)}) copy-start(bf16[64,2048]{1,0:T(8,128)(2,1)} %q_ref.1) | copy-start | bytes 786436
  1.6 0.9 %copy-start.1 = (bf16[64,2048]{1,0:T(8,128)(2,1)S(1)}, bf16[64,2048]{1,0:T(8,128)(2,1)}, u32[]{:S(2)}) copy-start(bf16[64,2048]{1,0:T(8,128)(2,1)} %g_ref.1) | copy-start | bytes 786436
  2.5 0.9 %copy-start.2 = (s32[49152]{0:T(1024)S(1)}, s32[49152]{0:T(1024)}, u32[]{:S(2)}) copy-start(s32[49152]{0:T(1024)} %param.9) | copy-start | bytes 589828
  3.5 0.9 %copy-start.3 = (bf16[64,1024]{1,0:T(8,128)(2,1)S(1)}, bf16[64,1024]{1,0:T(8,128)(2,1)}, u32[]{:S(2)}) copy-start(bf16[64,1024]{1,0:T(8,128)(2,1)} %k_ref.1) | copy-start | bytes 393220
  4.4 0.9 %copy-start.4 = (bf16[64,1024]{1,0:T(8,128)(2,1)S(1)}, bf16[64,1024]{1,0:T(8,128)(2,1)}, u32[]{:S(2)}) copy-start(bf16[64,1024]{1,0:T(8,128)(2,1)} %v_ref.1) | copy-start | bytes 393220

commit v2 on v1

v2 whole, which is shorter than its diff:
```python
import functools
import math

import jax
import jax.numpy as jnp
from jax import lax
from jax.experimental import pallas as pl
from jax.experimental.pallas import tpu as pltpu
from jax.sharding import PartitionSpec as P

MESH = pl.DeviceIdType.MESH
D = 128
WINDOW = 1024
SCALE = 168.0 ** -0.5
C2 = SCALE * math.log2(math.e)
NEG = -1e30
F32 = jnp.float32
BF16 = jnp.bfloat16
B = 256
PIECE = 64
TILES = 5


def dot_nt(a, b):
    return lax.dot_general(a, b, (((1,), (1,)), ((), ())), preferred_element_type=F32)


def dot_nn(a, b):
    return jnp.dot(a, b, preferred_element_type=F32)


def wide(x):
    return jnp.concatenate([x, x], axis=1)


def kernel(pipe, q_ref, k_ref, v_ref, g_ref, seg_hbm, o_out, dq_out, dk_out, dv_out,
           seg_ref, qst, gst, kbuf, vbuf, bias, pbuf, mtile, mrun, lrun, acc, delta,
           qT, gT, dkT, dvT, obuf, dqbuf, snd2, rcv2, snd1, rcv1, fin,
           seg_sem, in_send, in_recv, own_sem, halo_send, halo_recv, ret_send, ret_recv,
           out_send, out_recv, out_own):
    p = lax.axis_index("pipe")
    t = lax.axis_index("tensor")
    core = p % 2
    other = 1 - core
    chip = p // 2
    chips = pipe // 2
    nxt = ((p + 2) % pipe, t)
    prv = ((p + pipe - 2) % pipe, t)
    head = 2 * t + core
    has_prev, has_prev2, has_next = chip >= 1, chip >= 2, chip < chips - 1
    has_both = has_prev & has_next
    FAR = [(dx, c) for dx in (2, 1, 3) for c in range(2)]
    ALL = [(0, other)] + FAR

    seg_copy = pltpu.make_async_copy(seg_hbm, seg_ref, seg_sem)
    seg_copy.start()
    barrier = pltpu.get_barrier_semaphore()
    for dx, c in ALL:
        pl.semaphore_signal(barrier, inc=1, device_id=(chip * 2 + c, (t + dx) % 4), device_id_type=MESH)

    @pl.when(has_next)
    def _():
        pl.semaphore_signal(barrier, inc=1, device_id=nxt, device_id_type=MESH)

    @pl.when(has_prev)
    def _():
        pl.semaphore_signal(barrier, inc=1, device_id=prv, device_id_type=MESH)

    pl.semaphore_wait(barrier, 9 - (chip == 0).astype(jnp.int32) - (chip == chips - 1).astype(jnp.int32))

    def src_of(a, head_of):
        if a == 0:
            return k_ref.at[:, pl.ds(pl.multiple_of(head_of * D, D), D)]
        if a == 1:
            return v_ref.at[:, pl.ds(pl.multiple_of(head_of * D, D), D)]
        h = a % 2
        ref = q_ref if a < 4 else g_ref
        return ref.at[:, pl.ds(pl.multiple_of((2 * head_of + h) * D, D), D)]

    def dst_of(a, c, x):
        if a < 2:
            ref = kbuf if a == 0 else vbuf
            return ref.at[pl.ds(pl.multiple_of(4 * B + c * B + x * PIECE, PIECE), PIECE), :]
        h = a % 2
        ref = qst if a < 4 else gst
        return ref.at[c, pl.ds(pl.multiple_of(h * B + x * PIECE, PIECE), PIECE), :]

    def exchange(a, dx, c):
        x = (t + dx) % 4
        return pltpu.make_async_remote_copy(
            src_ref=src_of(a, 2 * x + c), dst_ref=dst_of(a, core, t),
            send_sem=in_send.at[a, dx, c], recv_sem=in_recv.at[a, dx, core],
            device_id=(chip * 2 + c, x), device_id_type=MESH)

    def exchanged(a, dx, c):
        x = (t + 4 - dx) % 4
        return pltpu.make_async_remote_copy(
            src_ref=src_of(a, head), dst_ref=dst_of(a, c, x),
            send_sem=in_send.at[a, dx, c], recv_sem=in_recv.at[a, dx, c],
            device_id=(chip * 2 + c, x), device_id_type=MESH)

    def own(a):
        return pltpu.make_async_copy(src_of(a, head), dst_of(a, core, t), own_sem.at[a])

    def rows_at(ref, block, c, x):
        return ref.at[pl.ds(pl.multiple_of(block * 2 * B + c * B + x * PIECE, PIECE), PIECE), :]

    def halo(hop, a, dx, c):
        x = (t + 4 - dx) % 4
        ref = kbuf if a == 0 else vbuf
        return pltpu.make_async_remote_copy(
            src_ref=rows_at(ref, 2 - hop, c, x), dst_ref=rows_at(ref, 1 - hop, c, x),
            send_sem=halo_send.at[hop, a, dx, c], recv_sem=halo_recv.at[hop, a, dx, c],
            device_id=nxt, device_id_type=MESH)

    for a in range(6):
        exchange(a, 0, other).start()
        own(a).start()
    for a in range(6):
        for dx, c in FAR:
            exchange(a, dx, c).start()

    def zero_block(block):
        kbuf[block * 2 * B:(block + 1) * 2 * B, :] = jnp.zeros((2 * B, D), BF16)
        vbuf[block * 2 * B:(block + 1) * 2 * B, :] = jnp.zeros((2 * B, D), BF16)

    @pl.when(chip == 0)
    def _():
        zero_block(1)

    @pl.when(chip <= 1)
    def _():
        zero_block(0)

    seg_copy.wait()

    row = lax.broadcasted_iota(jnp.int32, (B, D), 0)
    col = lax.broadcasted_iota(jnp.int32, (B, D), 1)

    def seg_row(r):
        at = chip * 4 - 8 + r
        s = seg_ref[pl.ds(jnp.maximum(at, 0), 1), :]
        return jnp.where(at >= 0, s, -1)

    for b in range(2):
        qcols = []
        for part in range(2):
            s = jnp.broadcast_to(seg_row(8 + 2 * b + part), (D, D))
            qcols.append(jnp.transpose(s))
        qseg = jnp.concatenate(qcols, axis=0)

        def mask_tile(l, carry):
            i = b + l
            for part in range(2):
                kseg = jnp.broadcast_to(seg_row(2 * i + part), (B, D))
                gap = row - col + (b * B + 4 * B - i * B - part * D)
                ok = (kseg == qseg) & (gap >= 0) & (gap < WINDOW)
                bias[b, l, :, part * D:(part + 1) * D] = jnp.where(ok, 0.0, NEG)
            return carry

        lax.fori_loop(0, TILES, mask_tile, 0)

    mrun[...] = jnp.full(mrun.shape, NEG, F32)
    lrun[...] = jnp.zeros(lrun.shape, F32)
    acc[...] = jnp.zeros(acc.shape, F32)

    NEAR = [(0, 0), (0, 1), (1, 0), (3, 0), (1, 1), (3, 1), (2, 0), (2, 1)]

    def arrived(a, dx, c):
        if dx == 0:
            @pl.when(core == c)
            def _():
                own(a).wait()

            @pl.when(core != c)
            def _():
                exchanged(a, 0, c).wait_recv()
        else:
            exchanged(a, dx, c).wait_recv()

    for a in range(2):
        for dx, c in NEAR:
            arrived(a, dx, c)

            @pl.when(has_next)
            def _():
                halo(0, a, dx, c).start()

    for c in (1, 0):
        for a in range(2):
            for dx in (0, 1, 3, 2):
                @pl.when(has_prev)
                def _():
                    halo(0, a, dx, c).wait_recv()

                @pl.when(has_both)
                def _():
                    halo(1, a, dx, c).start()

    def k_tile(i):
        return kbuf[pl.ds(pl.multiple_of(i * B, B), B), :]

    def v_tile(i):
        return vbuf[pl.ds(pl.multiple_of(i * B, B), B), :]

    def forward(b, i):
        l = i - b
        n = b * TILES + l
        s = dot_nt(qst[b], k_tile(i)) * C2
        bias_t = bias[b, l]
        s = s + jnp.concatenate([bias_t, bias_t], axis=0)
        m_old = mrun[b]
        m_new = jnp.maximum(m_old, jnp.max(s, axis=1, keepdims=True))
        e = jnp.exp2(s - wide(m_new))
        alpha = jnp.exp2(m_old - m_new)
        mrun[b] = m_new
        mtile[n] = m_new
        lrun[b] = lrun[b] * alpha + jnp.sum(e, axis=1, keepdims=True)
        e16 = e.astype(BF16)
        pbuf[n] = e16
        acc[b] = acc[b] * alpha + dot_nn(e16, v_tile(i))

    for a in (2, 3):
        for dx, c in NEAR:
            arrived(a, dx, c)

    def phase1(n, carry):
        forward(jnp.minimum(n, 1), 4 + n % 2)
        return carry

    lax.fori_loop(0, 3, phase1, 0)

    def phase2(n, carry):
        forward(n // 2, 3 - n % 2)
        return carry

    lax.fori_loop(0, 4, phase2, 0)
    for a in (4, 5):
        for dx, c in NEAR:
            arrived(a, dx, c)
    for b in range(2):
        qT[b] = jnp.transpose(qst[b].astype(F32)).astype(BF16)
        gT[b] = jnp.transpose(gst[b].astype(F32)).astype(BF16)
    dkT[...] = jnp.zeros(dkT.shape, F32)
    dvT[...] = jnp.zeros(dvT.shape, F32)

    def finish(b):
        linv = 1.0 / lrun[b]
        lrun[b] = linv
        o16 = (acc[b] * linv).astype(BF16)
        obuf[b] = o16
        d = jnp.sum(gst[b].astype(F32) * o16.astype(F32), axis=1, keepdims=True)
        delta[b] = jnp.broadcast_to(d, (2 * B, D))
        acc[b] = jnp.zeros((2 * B, D), F32)

    for c in (1, 0):
        @pl.when(has_prev2)
        def _():
            for a in range(2):
                for dx in range(4):
                    halo(1, a, dx, c).wait_recv()

        if c == 1:
            def phase3(n, carry):
                forward(n, 1)
                return carry

            lax.fori_loop(0, 2, phase3, 0)
            finish(1)
        else:
            forward(0, 0)
            finish(0)

    def out_src(a, c, x):
        if a < 4:
            ref = obuf if a < 2 else dqbuf
            return ref.at[c, pl.ds(pl.multiple_of((a % 2) * B + x * PIECE, PIECE), PIECE), :]
        return fin.at[a - 4, c, pl.ds(pl.multiple_of(x * PIECE, PIECE), PIECE), :]

    def out_dst(a, head_of):
        if a < 4:
            ref = o_out if a < 2 else dq_out
            return ref.at[:, pl.ds(pl.multiple_of((2 * head_of + a % 2) * D, D), D)]
        ref = dk_out if a == 4 else dv_out
        return ref.at[:, pl.ds(pl.multiple_of(head_of * D, D), D)]

    def give(a, dx, c):
        x = (t + dx) % 4
        return pltpu.make_async_remote_copy(
            src_ref=out_src(a, c, x), dst_ref=out_dst(a, head),
            send_sem=out_send.at[a, dx, c], recv_sem=out_recv.at[a, dx, core],
            device_id=(chip * 2 + c, x), device_id_type=MESH)

    def given(a, dx, c):
        x = (t + 4 - dx) % 4
        return pltpu.make_async_remote_copy(
            src_ref=out_src(a, core, t), dst_ref=out_dst(a, 2 * x + c),
            send_sem=out_send.at[a, dx, c], recv_sem=out_recv.at[a, dx, c],
            device_id=(chip * 2 + c, x), device_id_type=MESH)

    def keep(a):
        return pltpu.make_async_copy(out_src(a, core, t), out_dst(a, head), out_own.at[a])

    def give_all(arrays):
        for a in arrays:
            for dx, c in FAR:
                give(a, dx, c).start()
            give(a, 0, other).start()
            keep(a).start()

    def backward(b, i):
        n = b * TILES + i - b
        r = jnp.exp2(mtile[n] - mrun[b]) * lrun[b]
        prob = pbuf[n].astype(F32) * wide(r)
        dp = dot_nt(gst[b], v_tile(i))
        ds = (prob * (dp - wide(delta[b]))).astype(BF16)
        dvT[i] += dot_nn(gT[b], prob.astype(BF16))
        dkT[i] += dot_nn(qT[b], ds)
        acc[b] += dot_nn(ds, k_tile(i))

    def back(hop, i, a):
        s, r = (snd2, rcv2) if hop == 0 else (snd1, rcv1)
        return pltpu.make_async_remote_copy(
            src_ref=s.at[i, a], dst_ref=r.at[i, a],
            send_sem=ret_send.at[hop, i, a], recv_sem=ret_recv.at[hop, i, a],
            device_id=prv, device_id_type=MESH)

    def send_back(hop, i):
        for a, ref in ((0, dkT), (1, dvT)):
            if hop == 0:
                snd2[i, a] = ref[i].astype(BF16)

                @pl.when(has_prev2)
                def _():
                    back(0, i, a).start()
            else:
                @pl.when(has_both)
                def _():
                    back(0, i, a).wait_recv()
                    snd1[i, a] = (ref[2 + i] + rcv2[i, a].astype(F32)).astype(BF16)

                @pl.when(chip == chips - 1)
                def _():
                    snd1[i, a] = ref[2 + i].astype(BF16)

                @pl.when(has_prev)
                def _():
                    back(1, i, a).start()

    def pair(n, carry):
        backward(n % 2, 1 + n // 2)
        return carry

    backward(0, 0)
    send_back(0, 0)
    lax.fori_loop(0, 2, pair, 0)
    send_back(0, 1)
    give_all((0, 1))
    lax.fori_loop(2, 4, pair, 0)
    send_back(1, 0)
    lax.fori_loop(4, 6, pair, 0)
    send_back(1, 1)
    lax.fori_loop(6, 8, pair, 0)
    backward(1, 5)
    for b in range(2):
        dqbuf[b] = (acc[b] * SCALE).astype(BF16)
    give_all((2, 3))

    for i in range(2):
        for a, ref in ((0, dkT), (1, dvT)):
            factor = SCALE if a == 0 else 1.0

            @pl.when(has_next)
            def _():
                back(1, i, a).wait_recv()
                fin[a, i] = jnp.transpose((ref[4 + i] + rcv1[i, a].astype(F32)) * factor).astype(BF16)

            @pl.when(chip == chips - 1)
            def _():
                fin[a, i] = jnp.transpose(ref[4 + i] * factor).astype(BF16)

            for dx in (2, 1, 3):
                give(4 + a, dx, i).start()
    for a in (4, 5):
        give(a, 0, other).start()
        keep(a).start()

    for a in range(6):
        for dx, c in ALL:
            exchange(a, dx, c).wait_send()
            give(a, dx, c).wait_send()
            given(a, dx, c).wait_recv()
        keep(a).wait()

    @pl.when(has_next)
    def _():
        for a in range(2):
            for dx, c in NEAR:
                halo(0, a, dx, c).wait_send()

    @pl.when(has_both)
    def _():
        for a in range(2):
            for dx, c in NEAR:
                halo(1, a, dx, c).wait_send()

    for hop, cond in ((0, has_prev2), (1, has_prev)):
        @pl.when(cond)
        def _():
            for a in range(2):
                for i in range(2):
                    back(hop, i, a).wait_send()


def write_kernel(*refs):
    sems = refs[-1]
    copies = [pltpu.make_async_copy(refs[i], refs[4 + i], sems.at[i]) for i in range(4)]
    for copy in copies:
        copy.start()
    for copy in copies:
        copy.wait()


def body(pipe, query, key, value, grad_out, segment_ids):
    seg = segment_ids.reshape(-1, D)
    anyspace = pl.BlockSpec(memory_space=pl.ANY)
    dma = pltpu.SemaphoreType.DMA
    hbm = pl.BlockSpec(memory_space=pltpu.HBM)
    shapes = tuple(jax.ShapeDtypeStruct(x.shape, BF16) for x in (query, query, key, value))
    results = pl.pallas_call(
        functools.partial(kernel, pipe),
        out_shape=shapes,
        in_specs=[hbm] * 5,
        out_specs=(anyspace,) * 4,
        scratch_shapes=[
            pltpu.VMEM(seg.shape, jnp.int32),
            pltpu.VMEM((2, 2 * B, D), BF16),
            pltpu.VMEM((2, 2 * B, D), BF16),
            pltpu.VMEM((6 * B, D), BF16),
            pltpu.VMEM((6 * B, D), BF16),
            pltpu.VMEM((2, TILES, B, B), F32),
            pltpu.VMEM((2 * TILES, 2 * B, B), BF16),
            pltpu.VMEM((2 * TILES, 2 * B, D), F32),
            pltpu.VMEM((2, 2 * B, D), F32),
            pltpu.VMEM((2, 2 * B, D), F32),
            pltpu.VMEM((2, 2 * B, D), F32),
            pltpu.VMEM((2, 2 * B, D), F32),
            pltpu.VMEM((2, D, 2 * B), BF16),
            pltpu.VMEM((2, D, 2 * B), BF16),
            pltpu.VMEM((6, D, B), F32),
            pltpu.VMEM((6, D, B), F32),
            pltpu.VMEM((2, 2 * B, D), BF16),
            pltpu.VMEM((2, 2 * B, D), BF16),
            pltpu.VMEM((2, 2, D, B), BF16),
            pltpu.VMEM((2, 2, D, B), BF16),
            pltpu.VMEM((2, 2, D, B), BF16),
            pltpu.VMEM((2, 2, D, B), BF16),
            pltpu.VMEM((2, 2, B, D), BF16),
            dma(()), dma((6, 4, 2)), dma((6, 4, 2)), dma((6,)),
            dma((2, 2, 4, 2)), dma((2, 2, 4, 2)),
            dma((2, 2, 2)), dma((2, 2, 2)),
            dma((6, 4, 2)), dma((6, 4, 2)), dma((6,)),
        ],
        compiler_params=pltpu.CompilerParams(
            collective_id=0, has_side_effects=True, vmem_limit_bytes=40 * 1024 * 1024),
    )(*[pltpu.with_memory_space_constraint(x, pltpu.HBM) for x in (query, key, value, grad_out, seg)])
    return pl.pallas_call(
        write_kernel,
        out_shape=shapes,
        in_specs=[pl.BlockSpec(memory_space=pltpu.VMEM)] * 4,
        out_specs=(hbm,) * 4,
        scratch_shapes=[dma((4,))],
    )(*[pltpu.with_memory_space_constraint(x, pltpu.VMEM) for x in results])


def solution(mesh):
    spec = P(("pipe", "tensor"), None)
    return jax.shard_map(
        functools.partial(body, mesh.shape["pipe"]),
        mesh=mesh,
        in_specs=(spec,) * 4 + (P(),),
        out_specs=(spec,) * 4,
        check_vma=False,
    )
```

time: 64.1 us -> 48.6 us (0.76)
  Pallas kernels: 55.8 us -> 47.8 us
  local copies, waits for them, and re-layouts: 7.34 us -> 0 us
    pallas_call x1 -> x2, Pallas kernels: 55.8 us -> 47.8 us  [the longest x1 46.9 us: body(): pl.pallas_call(functools.partial(kernel, pipe), out_shape=shapes, in_spec...]
    unnamed x14 -> x0, local copies, waits for them, and re-layouts: 7.34 us -> none
where the time goes in v2:
time: 48.6 us; the launch traced here: 48.4 us
  Pallas kernels  47.8 us (98%)
  between operations  0.64 us (1%)
    pallas_call x1, Pallas kernels, body(): pl.pallas_call(functools.partial(kernel, pipe), out_shape=shapes, in_spec...  46.9 us

profile of v2, /device:TPU:1, one launch (start us, length us, event | category | flops | bytes accessed | tf_op | source)
XLA Modules:
  0.0 48.4 jit_solution(9556747430972358262)
XLA Ops:
  0.6 46.9 %shard_map.84 = (bf16[64,2048]{1,0:T(8,128)(2,1)S(1)}, bf16[64,2048]{1,0:T(8,128)(2,1)S(1)}, bf16[64,1024]{1,0:T(8,128)(2,1)S(1)}, bf16[64,1024]{1,0:T(8,128)(2,1)S(1)}) custom-call(bf16[64,2048]{1,0:T(8,128)(2,1)} %q_ref.1, bf16[64,1024]{1,0:T(8,128)(2,1)} %k_ref.1, bf16[64,1024]{1,0:T(8,128)(2,1)} %v_ref.1, bf16[64,2048]{1,0:T(8,128)(2,1)} %g_ref.1, ...), custom_call_target="tpu_custom_call" | custom-call | tf_op jit(solution)/shard_map/pallas_call | solution.py:430
  47.5 0.9 %shard_map.85 = (bf16[64,2048]{1,0:T(8,128)(2,1)}, bf16[64,2048]{1,0:T(8,128)(2,1)}, bf16[64,1024]{1,0:T(8,128)(2,1)}, bf16[64,1024]{1,0:T(8,128)(2,1)}) custom-call(bf16[64,2048]{1,0:T(8,128)(2,1)S(1)} %get-tuple-element.8.refs_0_, bf16[64,2048]{1,0:T(8,128)(2,1)S(1)} %get-tuple-element.9.refs_1_, bf16[64,1024]{1,0:T(8,128)(2,1)S(1)} %get-tuple-element.10.refs_2_, ...), custom_call_target="tpu_custom_call" | custom-call | tf_op jit(solution)/shard_map/pallas_call | solution.py:467

commit v3 on v2

v3 whole, which is shorter than its diff:
```python
import functools
import math

import jax
import jax.numpy as jnp
from jax import lax
from jax.experimental import pallas as pl
from jax.experimental.pallas import tpu as pltpu
from jax.sharding import PartitionSpec as P

MESH = pl.DeviceIdType.MESH
D = 128
WINDOW = 1024
SCALE = 168.0 ** -0.5
C2 = SCALE * math.log2(math.e)
NEG = -1e30
F32 = jnp.float32
BF16 = jnp.bfloat16
B = 256
PIECE = 64
TILES = 5


def dot_nt(a, b):
    return lax.dot_general(a, b, (((1,), (1,)), ((), ())), preferred_element_type=F32)


def dot_nn(a, b):
    return jnp.dot(a, b, preferred_element_type=F32)


def wide(x):
    return jnp.concatenate([x, x], axis=1)


def kernel(pipe, q_ref, k_ref, v_ref, g_ref, seg_hbm, o_out, dq_out, dk_out, dv_out,
           seg_ref, qst, gst, kbuf, vbuf, bias, pbuf, mtile, mrun, lrun, acc, delta,
           qT, gT, dkT, dvT, obuf, dqbuf, snd, rcv, fin,
           seg_sem, in_send, in_recv, own_sem, hop_send, hop_recv,
           out_send, out_recv, out_own):
    p = lax.axis_index("pipe")
    t = lax.axis_index("tensor")
    core = p % 2
    other = 1 - core
    chip = p // 2
    chips = pipe // 2
    nxt = ((p + 2) % pipe, t)
    prv = ((p + pipe - 2) % pipe, t)
    head = 2 * t + core
    has_prev, has_prev2, has_next = chip >= 1, chip >= 2, chip < chips - 1
    has_both = has_prev & has_next
    first, last = chip == 0, chip == chips - 1
    FAR = [(dx, c) for dx in (2, 1, 3) for c in range(2)]
    ALL = [(0, other)] + FAR

    seg_copy = pltpu.make_async_copy(seg_hbm, seg_ref, seg_sem)
    seg_copy.start()
    barrier = pltpu.get_barrier_semaphore()
    for dx, c in ALL:
        pl.semaphore_signal(barrier, inc=1, device_id=(chip * 2 + c, (t + dx) % 4), device_id_type=MESH)

    @pl.when(has_next)
    def _():
        pl.semaphore_signal(barrier, inc=1, device_id=nxt, device_id_type=MESH)

    @pl.when(has_prev)
    def _():
        pl.semaphore_signal(barrier, inc=1, device_id=prv, device_id_type=MESH)

    pl.semaphore_wait(barrier, 9 - (chip == 0).astype(jnp.int32) - (chip == chips - 1).astype(jnp.int32))

    def src_of(a, head_of):
        if a == 0:
            return k_ref.at[:, pl.ds(pl.multiple_of(head_of * D, D), D)]
        if a == 1:
            return v_ref.at[:, pl.ds(pl.multiple_of(head_of * D, D), D)]
        h = a % 2
        ref = q_ref if a < 4 else g_ref
        return ref.at[:, pl.ds(pl.multiple_of((2 * head_of + h) * D, D), D)]

    def rows_at(ref, tile, x):
        return ref.at[pl.ds(pl.multiple_of(tile * B + x * PIECE, PIECE), PIECE), :]

    def heads_at(a, tile, x):
        ref = qst if a < 4 else gst
        return ref.at[tile, pl.ds(pl.multiple_of((a % 2) * B + x * PIECE, PIECE), PIECE), :]

    def dst_of(a, c, x):
        if a < 2:
            return rows_at(kbuf if a == 0 else vbuf, 3 + c, x)
        return heads_at(a, 2 - 2 * c, x)

    def exchange(a, dx, c):
        x = (t + dx) % 4
        return pltpu.make_async_remote_copy(
            src_ref=src_of(a, 2 * x + c), dst_ref=dst_of(a, core, t),
            send_sem=in_send.at[a, dx, c], recv_sem=in_recv.at[a, dx, core],
            device_id=(chip * 2 + c, x), device_id_type=MESH)

    def exchanged(a, dx, c):
        x = (t + 4 - dx) % 4
        return pltpu.make_async_remote_copy(
            src_ref=src_of(a, head), dst_ref=dst_of(a, c, x),
            send_sem=in_send.at[a, dx, c], recv_sem=in_recv.at[a, dx, c],
            device_id=(chip * 2 + c, x), device_id_type=MESH)

    def own(a):
        return pltpu.make_async_copy(src_of(a, head), dst_of(a, core, t), own_sem.at[a])

    def hop(at, src, dst, dev):
        return pltpu.make_async_remote_copy(
            src_ref=src, dst_ref=dst, send_sem=hop_send.at[at], recv_sem=hop_recv.at[at],
            device_id=dev, device_id_type=MESH)

    def up(a, dx, c):
        ref, x = kbuf if a == 0 else vbuf, (t + 4 - dx) % 4
        return hop(a * 8 + dx * 2 + c, rows_at(ref, 3 + c, x), rows_at(ref, 1 + c, x), nxt)

    def up2(a, dx):
        ref, x = kbuf if a == 0 else vbuf, (t + 4 - dx) % 4
        return hop(16 + a * 4 + dx, rows_at(ref, 2, x), rows_at(ref, 0, x), nxt)

    def down(a, dx):
        x = (t + 4 - dx) % 4
        if a < 2:
            ref = kbuf if a == 0 else vbuf
            return hop(24 + a * 4 + dx, rows_at(ref, 3, x), rows_at(ref, 5, x), prv)
        return hop(24 + a * 4 + dx, heads_at(a, 2, x), heads_at(a, 1, x), prv)

    for a in range(6):
        exchange(a, 0, other).start()
        own(a).start()
    for a in range(6):
        for dx, c in FAR:
            exchange(a, dx, c).start()

    def zero_tile(i):
        kbuf[i * B:(i + 1) * B, :] = jnp.zeros((B, D), BF16)
        vbuf[i * B:(i + 1) * B, :] = jnp.zeros((B, D), BF16)

    @pl.when(first)
    def _():
        zero_tile(1)
        zero_tile(2)

    @pl.when(chip <= 1)
    def _():
        zero_tile(0)

    @pl.when(last)
    def _():
        zero_tile(5)
        qst[1] = jnp.zeros((2 * B, D), BF16)
        gst[1] = jnp.zeros((2 * B, D), BF16)

    def arrived(a, dx, c):
        if dx == 0:
            @pl.when(core == c)
            def _():
                own(a).wait()

            @pl.when(core != c)
            def _():
                exchanged(a, 0, c).wait_recv()
        else:
            exchanged(a, dx, c).wait_recv()

    STEPS = (0, 1, 3, 2)

    def masks():
        row = lax.broadcasted_iota(jnp.int32, (B, D), 0)
        col = lax.broadcasted_iota(jnp.int32, (B, D), 1)

        def seg_row(at):
            inside = (at >= 0) & (at < 4 * chips)
            r = seg_ref[pl.ds(jnp.minimum(jnp.maximum(at, 0), 4 * chips - 1), 1), :]
            return jnp.where(inside, r, -1)

        def seg_col(at):
            parts = [jnp.transpose(jnp.broadcast_to(seg_row(at + k), (D, D))) for k in range(2)]
            return jnp.concatenate(parts, axis=0)

        def mask(b, l, at, offset, qseg):
            for part in range(2):
                kseg = jnp.broadcast_to(seg_row(at + part), (B, D))
                gap = row - col + (offset - part * D)
                ok = (kseg == qseg) & (gap >= 0) & (gap < WINDOW)
                bias[b, l, :, part * D:(part + 1) * D] = jnp.where(ok, 0.0, NEG)

        for b in range(2):
            qseg = seg_col(4 * chip + 2 + 2 * b)

            def mask_tile(l, carry):
                mask(b, l, 4 * chip - 6 + 2 * (b + l), 4 * B - l * B, qseg)
                return carry

            lax.fori_loop(0, TILES, mask_tile, 0)

        @pl.when(first)
        def _():
            mask(2, 1, 4 * chip, 0, seg_col(4 * chip))

    for c in (1, 0):
        for a in range(2):
            for dx in STEPS:
                arrived(a, dx, c)

                @pl.when(has_next)
                def _():
                    up(a, dx, c).start()

                if c == 0:
                    @pl.when(has_prev)
                    def _():
                        down(a, dx).start()
        if c == 1:
            seg_copy.wait()
            masks()

    mrun[...] = jnp.full(mrun.shape, NEG, F32)
    lrun[...] = jnp.zeros(lrun.shape, F32)
    acc[...] = jnp.zeros(acc.shape, F32)

    for a in range(2):
        for dx in STEPS:
            @pl.when(has_prev)
            def _():
                up(a, dx, 1).wait_recv()

            @pl.when(has_both)
            def _():
                up2(a, dx).start()

    def k_tile(i):
        return kbuf[pl.ds(pl.multiple_of(i * B, B), B), :]

    def v_tile(i):
        return vbuf[pl.ds(pl.multiple_of(i * B, B), B), :]

    def forward(b, i):
        l = i - b
        n = b * TILES + l
        s = dot_nt(qst[b], k_tile(i)) * C2
        bias_t = bias[b, l]
        s = s + jnp.concatenate([bias_t, bias_t], axis=0)
        m_old = mrun[b]
        m_new = jnp.maximum(m_old, jnp.max(s, axis=1, keepdims=True))
        e = jnp.exp2(s - wide(m_new))
        alpha = jnp.exp2(m_old - m_new)
        mrun[b] = m_new
        mtile[n] = m_new
        lrun[b] = lrun[b] * alpha + jnp.sum(e, axis=1, keepdims=True)
        e16 = e.astype(BF16)
        pbuf[n] = e16
        acc[b] = acc[b] * alpha + dot_nn(e16, v_tile(i))

    def local(arrays):
        for a in arrays:
            for dx in STEPS:
                arrived(a, dx, 0)

                @pl.when(has_prev)
                def _():
                    down(a, dx).start()

    def here(a):
        for dx in STEPS:
            arrived(a, dx, 1)

    local((2, 3))
    here(2)
    here(3)

    def two(b, i):
        def step(n, carry):
            forward(b, i - n)
            return carry

        lax.fori_loop(0, 2, step, 0)

    two(0, 4)
    local((4, 5))

    @pl.when(has_prev)
    def _():
        for a in range(2):
            for dx in STEPS:
                up(a, dx, 0).wait_recv()

    two(0, 2)
    here(4)
    here(5)
    dkT[...] = jnp.zeros(dkT.shape, F32)
    dvT[...] = jnp.zeros(dvT.shape, F32)

    def turned(b):
        qT[b] = jnp.transpose(qst[b].astype(F32)).astype(BF16)
        gT[b] = jnp.transpose(gst[b].astype(F32)).astype(BF16)

    turned(0)

    def finish(b):
        linv = 1.0 / lrun[b]
        lrun[b] = linv
        o16 = (acc[b] * linv).astype(BF16)
        obuf[b] = o16
        d = jnp.sum(gst[b].astype(F32) * o16.astype(F32), axis=1, keepdims=True)
        delta[b] = jnp.broadcast_to(d, (2 * B, D))
        acc[b] = jnp.zeros((2 * B, D), F32)

    @pl.when(has_prev2)
    def _():
        for a in range(2):
            for dx in STEPS:
                up2(a, dx).wait_recv()

    forward(0, 0)
    finish(0)

    def out_src(a, c, x):
        if a < 4:
            ref = obuf if a < 2 else dqbuf
            return ref.at[2 - 2 * c, pl.ds(pl.multiple_of((a % 2) * B + x * PIECE, PIECE), PIECE), :]
        return fin.at[a - 4, c, pl.ds(pl.multiple_of(x * PIECE, PIECE), PIECE), :]

    def out_dst(a, head_of):
        if a < 4:
            ref = o_out if a < 2 else dq_out
            return ref.at[:, pl.ds(pl.multiple_of((2 * head_of + a % 2) * D, D), D)]
        ref = dk_out if a == 4 else dv_out
        return ref.at[:, pl.ds(pl.multiple_of(head_of * D, D), D)]

    def give(a, dx, c):
        x = (t + dx) % 4
        return pltpu.make_async_remote_copy(
            src_ref=out_src(a, c, x), dst_ref=out_dst(a, head),
            send_sem=out_send.at[a, dx, c], recv_sem=out_recv.at[a, dx, core],
            device_id=(chip * 2 + c, x), device_id_type=MESH)

    def given(a, dx, c):
        x = (t + 4 - dx) % 4
        return pltpu.make_async_remote_copy(
            src_ref=out_src(a, core, t), dst_ref=out_dst(a, 2 * x + c),
            send_sem=out_send.at[a, dx, c], recv_sem=out_recv.at[a, dx, c],
            device_id=(chip * 2 + c, x), device_id_type=MESH)

    def keep(a):
        return pltpu.make_async_copy(out_src(a, core, t), out_dst(a, head), out_own.at[a])

    def give_tile(a, c):
        for dx in (2, 1, 3):
            give(a, dx, c).start()

        @pl.when(core == c)
        def _():
            keep(a).start()

        @pl.when(core != c)
        def _():
            give(a, 0, c).start()

    def backward(b, i):
        n = b * TILES + i - b
        r = jnp.exp2(mtile[n] - mrun[b]) * lrun[b]
        prob = pbuf[n].astype(F32) * wide(r)
        dp = dot_nt(gst[b], v_tile(i))
        ds = (prob * (dp - wide(delta[b]))).astype(BF16)
        dvT[i] += dot_nn(gT[b], prob.astype(BF16))
        dkT[i] += dot_nn(qT[b], ds)
        acc[b] += dot_nn(ds, k_tile(i))

    def back(m, a):
        return hop(48 + 2 * m + a, snd.at[m, a], rcv.at[m, a], nxt if m == 3 else prv)

    def ahead(a):
        ref = obuf if a == 0 else dqbuf
        return hop(56 + a, ref.at[1], ref.at[2], nxt)

    def send_back(m, i, cond):
        for a, ref in ((0, dkT), (1, dvT)):
            snd[m, a] = ref[i].astype(BF16)

            @pl.when(cond)
            def _():
                back(m, a).start()

    backward(0, 0)
    send_back(0, 0, has_prev2)
    give_tile(0, 1)
    give_tile(1, 1)

    @pl.when(has_next)
    def _():
        for a in range(4):
            for dx in STEPS:
                down(a, dx).wait_recv()

    def late(n, carry):
        forward(1, 5 - n)
        return carry

    lax.fori_loop(0, TILES, late, 0)

    @pl.when(has_next)
    def _():
        for a in (4, 5):
            for dx in STEPS:
                down(a, dx).wait_recv()

    finish(1)

    @pl.when(has_next)
    def _():
        ahead(0).start()

    turned(1)
    backward(1, 5)
    send_back(3, 5, has_next)

    def both(n, carry):
        backward(n, 1)
        return carry

    lax.fori_loop(0, 2, both, 0)
    send_back(1, 1, has_prev)

    def rest(n, carry):
        backward(1, 2 + n)
        return carry

    lax.fori_loop(0, 3, rest, 0)
    dqbuf[1] = (acc[1] * SCALE).astype(BF16)

    @pl.when(has_next)
    def _():
        ahead(1).start()

    backward(0, 2)
    for a, ref in ((0, dkT), (1, dvT)):
        @pl.when(has_both)
        def _():
            back(0, a).wait_recv()
            snd[2, a] = (ref[2] + rcv[0, a].astype(F32)).astype(BF16)

        @pl.when(last)
        def _():
            snd[2, a] = ref[2].astype(BF16)

        @pl.when(has_prev)
        def _():
            back(2, a).start()

    def tail(n, carry):
        backward(0, 3 + n)
        return carry

    lax.fori_loop(0, 2, tail, 0)
    dqbuf[0] = (acc[0] * SCALE).astype(BF16)
    give_tile(2, 1)
    give_tile(3, 1)

    @pl.when(first)
    def _():
        forward(2, 3)
        finish(2)
        turned(2)
        backward(2, 3)
        dqbuf[2] = (acc[2] * SCALE).astype(BF16)

    @pl.when(has_prev)
    def _():
        ahead(0).wait_recv()

    give_tile(0, 0)
    give_tile(1, 0)
    for i in range(2):
        for a, ref in ((0, dkT), (1, dvT)):
            if i == 0:
                @pl.when(has_next)
                def _():
                    back(1, a).wait_recv()
                    ref[3] = ref[3] + rcv[1, a].astype(F32)

                @pl.when(has_prev)
                def _():
                    back(3, a).wait_recv()
                    ref[3] = ref[3] + rcv[3, a].astype(F32)
            else:
                @pl.when(has_next)
                def _():
                    back(2, a).wait_recv()
                    ref[4] = ref[4] + rcv[2, a].astype(F32)

            fin[a, i] = jnp.transpose(ref[3 + i] * (SCALE if a == 0 else 1.0)).astype(BF16)
            give_tile(4 + a, i)

    @pl.when(has_prev)
    def _():
        ahead(1).wait_recv()

    give_tile(2, 0)
    give_tile(3, 0)

    for a in range(6):
        for dx, c in ALL:
            exchange(a, dx, c).wait_send()
            give(a, dx, c).wait_send()
            given(a, dx, c).wait_recv()
        keep(a).wait()

    @pl.when(has_next)
    def _():
        for a in range(2):
            for dx in STEPS:
                for c in range(2):
                    up(a, dx, c).wait_send()
            back(3, a).wait_send()
            ahead(a).wait_send()

    @pl.when(has_both)
    def _():
        for a in range(2):
            for dx in STEPS:
                up2(a, dx).wait_send()

    @pl.when(has_prev)
    def _():
        for a in range(6):
            for dx in STEPS:
                down(a, dx).wait_send()
        for a in range(2):
            back(1, a).wait_send()
            back(2, a).wait_send()

    @pl.when(has_prev2)
    def _():
        for a in range(2):
            back(0, a).wait_send()


def write_kernel(*refs):
    sems = refs[-1]
    copies = [pltpu.make_async_copy(refs[i], refs[4 + i], sems.at[i]) for i in range(4)]
    for copy in copies:
        copy.start()
    for copy in copies:
        copy.wait()


def body(pipe, query, key, value, grad_out, segment_ids):
    seg = segment_ids.reshape(-1, D)
    anyspace = pl.BlockSpec(memory_space=pl.ANY)
    dma = pltpu.SemaphoreType.DMA
    hbm = pl.BlockSpec(memory_space=pltpu.HBM)
    shapes = tuple(jax.ShapeDtypeStruct(x.shape, BF16) for x in (query, query, key, value))
    results = pl.pallas_call(
        functools.partial(kernel, pipe),
        out_shape=shapes,
        in_specs=[hbm] * 5,
        out_specs=(anyspace,) * 4,
        scratch_shapes=[
            pltpu.VMEM(seg.shape, jnp.int32),
            pltpu.VMEM((3, 2 * B, D), BF16),
            pltpu.VMEM((3, 2 * B, D), BF16),
            pltpu.VMEM((6 * B, D), BF16),
            pltpu.VMEM((6 * B, D), BF16),
            pltpu.VMEM((3, TILES, B, B), F32),
            pltpu.VMEM((3 * TILES, 2 * B, B), BF16),
            pltpu.VMEM((3 * TILES, 2 * B, D), F32),
            pltpu.VMEM((3, 2 * B, D), F32),
            pltpu.VMEM((3, 2 * B, D), F32),
            pltpu.VMEM((3, 2 * B, D), F32),
            pltpu.VMEM((3, 2 * B, D), F32),
            pltpu.VMEM((3, D, 2 * B), BF16),
            pltpu.VMEM((3, D, 2 * B), BF16),
            pltpu.VMEM((6, D, B), F32),
            pltpu.VMEM((6, D, B), F32),
            pltpu.VMEM((3, 2 * B, D), BF16),
            pltpu.VMEM((3, 2 * B, D), BF16),
            pltpu.VMEM((4, 2, D, B), BF16),
            pltpu.VMEM((4, 2, D, B), BF16),
            pltpu.VMEM((2, 2, B, D), BF16),
            dma(()), dma((6, 4, 2)), dma((6, 4, 2)), dma((6,)),
            dma((58,)), dma((58,)),
            dma((6, 4, 2)), dma((6, 4, 2)), dma((6,)),
        ],
        compiler_params=pltpu.CompilerParams(
            collective_id=0, has_side_effects=True, vmem_limit_bytes=40 * 1024 * 1024),
    )(*[pltpu.with_memory_space_constraint(x, pltpu.HBM) for x in (query, key, value, grad_out, seg)])
    return pl.pallas_call(
        write_kernel,
        out_shape=shapes,
        in_specs=[pl.BlockSpec(memory_space=pltpu.VMEM)] * 4,
        out_specs=(hbm,) * 4,
        scratch_shapes=[dma((4,))],
    )(*[pltpu.with_memory_space_constraint(x, pltpu.VMEM) for x in results])


def solution(mesh):
    spec = P(("pipe", "tensor"), None)
    return jax.shard_map(
        functools.partial(body, mesh.shape["pipe"]),
        mesh=mesh,
        in_specs=(spec,) * 4 + (P(),),
        out_specs=(spec,) * 4,
        check_vma=False,
    )
```

time: 48.6 us -> 45.6 us (0.938)
  Pallas kernels: 47.8 us -> 44.4 us
    pallas_call x1, Pallas kernels: 46.9 us -> 43.5 us  [body(): pl.pallas_call(functools.partial(kernel, pipe), out_shape=shapes, in_spec...]
where the time goes in v3:
time: 45.6 us; the launch traced here: 45.1 us
  Pallas kernels  44.4 us (97%)
  between operations  0.64 us (1%)
    pallas_call x1, Pallas kernels, body(): pl.pallas_call(functools.partial(kernel, pipe), out_shape=shapes, in_spec...  43.5 us

profile of v3, /device:TPU:1, one launch (start us, length us, event | category | flops | bytes accessed | tf_op | source)
XLA Modules:
  0.0 45.1 jit_solution(7564096894586578952)
XLA Ops:
  0.6 43.5 %shard_map.84 = (bf16[64,2048]{1,0:T(8,128)(2,1)S(1)}, bf16[64,2048]{1,0:T(8,128)(2,1)S(1)}, bf16[64,1024]{1,0:T(8,128)(2,1)S(1)}, bf16[64,1024]{1,0:T(8,128)(2,1)S(1)}) custom-call(bf16[64,2048]{1,0:T(8,128)(2,1)} %q_ref.1, bf16[64,1024]{1,0:T(8,128)(2,1)} %k_ref.1, bf16[64,1024]{1,0:T(8,128)(2,1)} %v_ref.1, bf16[64,2048]{1,0:T(8,128)(2,1)} %g_ref.1, ...), custom_call_target="tpu_custom_call" | custom-call | tf_op jit(solution)/shard_map/pallas_call | solution.py:556
  44.2 0.9 %shard_map.85 = (bf16[64,2048]{1,0:T(8,128)(2,1)}, bf16[64,2048]{1,0:T(8,128)(2,1)}, bf16[64,1024]{1,0:T(8,128)(2,1)}, bf16[64,1024]{1,0:T(8,128)(2,1)}) custom-call(bf16[64,2048]{1,0:T(8,128)(2,1)S(1)} %get-tuple-element.8.refs_0_, bf16[64,2048]{1,0:T(8,128)(2,1)S(1)} %get-tuple-element.9.refs_1_, bf16[64,1024]{1,0:T(8,128)(2,1)S(1)} %get-tuple-element.10.refs_2_, ...), custom_call_target="tpu_custom_call" | custom-call | tf_op jit(solution)/shard_map/pallas_call | solution.py:590

commit v4 on v3

--- a/solution.py
+++ b/solution.py
@@ -37,7 +37,7 @@
            seg_ref, qst, gst, kbuf, vbuf, bias, pbuf, mtile, mrun, lrun, acc, delta,
            qT, gT, dkT, dvT, obuf, dqbuf, snd, rcv, fin,
            seg_sem, in_send, in_recv, own_sem, hop_send, hop_recv,
-           out_send, out_recv, out_own):
+           out_send, out_recv, out_own, ready):
     p = lax.axis_index("pipe")
     t = lax.axis_index("tensor")
     core = p % 2
@@ -56,18 +56,47 @@
     seg_copy = pltpu.make_async_copy(seg_hbm, seg_ref, seg_sem)
     seg_copy.start()
     barrier = pltpu.get_barrier_semaphore()
-    for dx, c in ALL:
-        pl.semaphore_signal(barrier, inc=1, device_id=(chip * 2 + c, (t + dx) % 4), device_id_type=MESH)
-
-    @pl.when(has_next)
-    def _():
-        pl.semaphore_signal(barrier, inc=1, device_id=nxt, device_id_type=MESH)
-
-    @pl.when(has_prev)
-    def _():
-        pl.semaphore_signal(barrier, inc=1, device_id=prv, device_id_type=MESH)
-
-    pl.semaphore_wait(barrier, 9 - (chip == 0).astype(jnp.int32) - (chip == chips - 1).astype(jnp.int32))
+    def greet(chip_of, c, x):
+        pl.semaphore_signal(barrier, inc=1, device_id=(chip_of * 2 + c, x), device_id_type=MESH)
+
+    origin = first & (core == 0) & (t == 0)
+    near_origin = (first & jnp.logical_not(origin)) | ((chip == 1) & (core == 0))
+
+    @pl.when(jnp.logical_not(origin))
+    def _():
+        for dx, c in ALL:
+            greet(chip, c, (t + dx) % 4)
+
+        @pl.when(has_next)
+        def _():
+            for x in range(4):
+                greet(chip + 1, 0, x)
+
+            @pl.when(core == 1)
+            def _():
+                greet(chip + 1, 1, t)
+
+        @pl.when(has_prev)
+        def _():
+            @pl.when(core == 0)
+            def _():
+                for x in range(4):
+                    for c in range(2):
+                        greet(chip - 1, c, x)
+
+            @pl.when(core == 1)
+            def _():
+                greet(chip - 1, 1, t)
+
+    n_prev, n_next = jnp.minimum(chip, 1), jnp.minimum(chips - 1 - chip, 1)
+    pl.semaphore_wait(barrier, 7 + n_next * (4 + core) + n_prev * (8 - 7 * core) - near_origin.astype(jnp.int32))
+
+    @pl.when(origin)
+    def _():
+        for dx, c in ALL:
+            pl.semaphore_signal(ready, inc=1, device_id=(c, dx % 4), device_id_type=MESH)
+        for x in range(4):
+            pl.semaphore_signal(ready, inc=1, device_id=(2, x), device_id_type=MESH)
 
     def src_of(a, head_of):
         if a == 0:
@@ -85,27 +114,37 @@
         ref = qst if a < 4 else gst
         return ref.at[tile, pl.ds(pl.multiple_of((a % 2) * B + x * PIECE, PIECE), PIECE), :]
 
-    def dst_of(a, c, x):
-        if a < 2:
-            return rows_at(kbuf if a == 0 else vbuf, 3 + c, x)
-        return heads_at(a, 2 - 2 * c, x)
+    shift = (1 - core) * n_prev
+    tile_to = (1 - core) * (2 - n_prev)
 
     def exchange(a, dx, c):
         x = (t + dx) % 4
+        if a < 2:
+            dst, mark, chip_to = rows_at(kbuf if a == 0 else vbuf, 3 + core, t), core, chip
+        else:
+            dst, mark, chip_to = heads_at(a, tile_to, t), tile_to, chip - shift
         return pltpu.make_async_remote_copy(
-            src_ref=src_of(a, 2 * x + c), dst_ref=dst_of(a, core, t),
-            send_sem=in_send.at[a, dx, c], recv_sem=in_recv.at[a, dx, core],
-            device_id=(chip * 2 + c, x), device_id_type=MESH)
-
-    def exchanged(a, dx, c):
+            src_ref=src_of(a, 2 * x + c), dst_ref=dst,
+            send_sem=in_send.at[a, dx, c], recv_sem=in_recv.at[a, dx, mark],
+            device_id=(chip_to * 2 + c, x), device_id_type=MESH)
+
+    def exchanged(a, dx, mark):
         x = (t + 4 - dx) % 4
+        if a < 2:
+            dst = rows_at(kbuf if a == 0 else vbuf, 3 + mark, x)
+        else:
+            dst = heads_at(a, mark, x)
         return pltpu.make_async_remote_copy(
-            src_ref=src_of(a, head), dst_ref=dst_of(a, c, x),
-            send_sem=in_send.at[a, dx, c], recv_sem=in_recv.at[a, dx, c],
-            device_id=(chip * 2 + c, x), device_id_type=MESH)
+            src_ref=src_of(a, head), dst_ref=dst,
+            send_sem=in_send.at[a, dx, 0], recv_sem=in_recv.at[a, dx, mark],
+            device_id=nxt, device_id_type=MESH)
 
     def own(a):
-        return pltpu.make_async_copy(src_of(a, head), dst_of(a, core, t), own_sem.at[a])
+        if a < 2:
+            dst = rows_at(kbuf if a == 0 else vbuf, 3 + core, t)
+        else:
+            dst = heads_at(a, tile_to, t)
+        return pltpu.make_async_copy(src_of(a, head), dst, own_sem.at[a])
 
     def hop(at, src, dst, dev):
         return pltpu.make_async_remote_copy(
@@ -121,18 +160,39 @@
         return hop(16 + a * 4 + dx, rows_at(ref, 2, x), rows_at(ref, 0, x), nxt)
 
     def down(a, dx):
-        x = (t + 4 - dx) % 4
+        ref, x = kbuf if a == 0 else vbuf, (t + 4 - dx) % 4
+        return hop(24 + a * 4 + dx, rows_at(ref, 3, x), rows_at(ref, 5, x), prv)
+
+    above_origin = (chip == 1) & (core == 0) & (t == 0)
+
+    def to_origin(a, dx, c):
+        chip_to = chip if a < 2 else chip - shift
+        return (chip_to == 0) & ((t + dx) % 4 == 0) & (c == 0)
+
+    for a in range(6):
+        @pl.when(jnp.logical_not(to_origin(a, 0, other)))
+        def _():
+            exchange(a, 0, other).start()
+
         if a < 2:
-            ref = kbuf if a == 0 else vbuf
-            return hop(24 + a * 4 + dx, rows_at(ref, 3, x), rows_at(ref, 5, x), prv)
-        return hop(24 + a * 4 + dx, heads_at(a, 2, x), heads_at(a, 1, x), prv)
-
-    for a in range(6):
-        exchange(a, 0, other).start()
-        own(a).start()
+            own(a).start()
+        else:
+            @pl.when(shift == 0)
+            def _():
+                own(a).start()
+
+            @pl.when((shift == 1) & jnp.logical_not(to_origin(a, 0, core)))
+            def _():
+                exchange(a, 0, core).start()
+
     for a in range(6):
         for dx, c in FAR:
-            exchange(a, dx, c).start()
+            if c == 0:
+                @pl.when(jnp.logical_not(to_origin(a, dx, c)))
+                def _():
+                    exchange(a, dx, c).start()
+            else:
+                exchange(a, dx, c).start()
 
     def zero_tile(i):
         kbuf[i * B:(i + 1) * B, :] = jnp.zeros((B, D), BF16)
@@ -154,6 +214,7 @@
         gst[1] = jnp.zeros((2 * B, D), BF16)
 
     def arrived(a, dx, c):
+        mark = c if a < 2 else 2 - 2 * c
         if dx == 0:
             @pl.when(core == c)
             def _():
@@ -161,9 +222,9 @@
 
             @pl.when(core != c)
             def _():
-                exchanged(a, 0, c).wait_recv()
+                exchanged(a, 0, mark).wait_recv()
         else:
-            exchanged(a, dx, c).wait_recv()
+            exchanged(a, dx, mark).wait_recv()
 
     STEPS = (0, 1, 3, 2)
 
@@ -200,26 +261,57 @@
         def _():
             mask(2, 1, 4 * chip, 0, seg_col(4 * chip))
 
-    for c in (1, 0):
-        for a in range(2):
-            for dx in STEPS:
-                arrived(a, dx, c)
-
-                @pl.when(has_next)
-                def _():
-                    up(a, dx, c).start()
-
-                if c == 0:
-                    @pl.when(has_prev)
-                    def _():
-                        down(a, dx).start()
-        if c == 1:
-            seg_copy.wait()
-            masks()
-
+    seg_copy.wait()
+    masks()
     mrun[...] = jnp.full(mrun.shape, NEG, F32)
     lrun[...] = jnp.zeros(lrun.shape, F32)
     acc[...] = jnp.zeros(acc.shape, F32)
+    dkT[...] = jnp.zeros(dkT.shape, F32)
+    dvT[...] = jnp.zeros(dvT.shape, F32)
+
+    for a in range(2):
+        for dx in STEPS:
+            arrived(a, dx, 1)
+
+            @pl.when(has_next)
+            def _():
+                up(a, dx, 1).start()
+
+    for a in range(2):
+        for dx in STEPS:
+            @pl.when(has_prev | (dx != t) | origin)
+            def _():
+                arrived(a, dx, 0)
+
+                @pl.when(has_next)
+                def _():
+                    up(a, dx, 0).start()
+
+                @pl.when(has_prev & jnp.logical_not(above_origin))
+                def _():
+                    down(a, dx).start()
+
+    def arrived_first(a):
+        exchanged(a, t, 0).wait_recv()
+
+    @pl.when(near_origin)
+    def _():
+        pl.semaphore_wait(ready, 1)
+        steps = (4 - t) % 4
+
+        @pl.when(first)
+        def _():
+            for a in range(2):
+                exchange(a, steps, 0).start()
+
+        for a in range(2, 6):
+            exchange(a, steps, 0).start()
+
+        @pl.when(above_origin)
+        def _():
+            for a in range(2):
+                for dx in STEPS:
+                    down(a, dx).start()
 
     for a in range(2):
         for dx in STEPS:
@@ -254,44 +346,26 @@
         pbuf[n] = e16
         acc[b] = acc[b] * alpha + dot_nn(e16, v_tile(i))
 
-    def local(arrays):
-        for a in arrays:
-            for dx in STEPS:
-                arrived(a, dx, 0)
-
-                @pl.when(has_prev)
-                def _():
-                    down(a, dx).start()
-
     def here(a):
         for dx in STEPS:
             arrived(a, dx, 1)
 
-    local((2, 3))
     here(2)
     here(3)
-
-    def two(b, i):
+    n_first = 1 - n_prev
+    early_tile, late_tile = 3 - 2 * n_first, 1 + 2 * n_first
+
+    def early(b, diagonal):
         def step(n, carry):
-            forward(b, i - n)
+            forward(b, jnp.where(n < 2, diagonal - n, jnp.where(n == 2, early_tile, 2)) if b else
+                    jnp.where(n == 0, 4, jnp.where(n == 1, early_tile, 2)))
             return carry
 
-        lax.fori_loop(0, 2, step, 0)
-
-    two(0, 4)
-    local((4, 5))
-
-    @pl.when(has_prev)
-    def _():
-        for a in range(2):
-            for dx in STEPS:
-                up(a, dx, 0).wait_recv()
-
-    two(0, 2)
+        lax.fori_loop(0, 4 if b else 3, step, 0)
+
+    early(0, 4)
     here(4)
     here(5)
-    dkT[...] = jnp.zeros(dkT.shape, F32)
-    dvT[...] = jnp.zeros(dvT.shape, F32)
 
     def turned(b):
         qT[b] = jnp.transpose(qst[b].astype(F32)).astype(BF16)
@@ -308,19 +382,11 @@
         delta[b] = jnp.broadcast_to(d, (2 * B, D))
         acc[b] = jnp.zeros((2 * B, D), F32)
 
-    @pl.when(has_prev2)
-    def _():
-        for a in range(2):
-            for dx in STEPS:
-                up2(a, dx).wait_recv()
-
-    forward(0, 0)
-    finish(0)
-
-    def out_src(a, c, x):
-        if a < 4:
-            ref = obuf if a < 2 else dqbuf
-            return ref.at[2 - 2 * c, pl.ds(pl.multiple_of((a % 2) * B + x * PIECE, PIECE), PIECE), :]
+    def heads_out(a, tile, x):
+        ref = obuf if a < 2 else dqbuf
+        return ref.at[tile, pl.ds(pl.multiple_of((a % 2) * B + x * PIECE, PIECE), PIECE), :]
+
+    def fin_at(a, c, x):
         return fin.at[a - 4, c, pl.ds(pl.multiple_of(x * PIECE, PIECE), PIECE), :]
 
     def out_dst(a, head_of):
@@ -330,34 +396,43 @@
         ref = dk_out if a == 4 else dv_out
         return ref.at[:, pl.ds(pl.multiple_of(head_of * D, D), D)]
 
-    def give(a, dx, c):
+    def give(a, dx, part):
         x = (t + dx) % 4
+        if a < 4:
+            src, dev = heads_out(a, part, x), ((chip + part % 2) * 2 + (1 if part == 0 else 0), x)
+        else:
+            src, dev = fin_at(a, part, x), (chip * 2 + part, x)
         return pltpu.make_async_remote_copy(
-            src_ref=out_src(a, c, x), dst_ref=out_dst(a, head),
-            send_sem=out_send.at[a, dx, c], recv_sem=out_recv.at[a, dx, core],
-            device_id=(chip * 2 + c, x), device_id_type=MESH)
+            src_ref=src, dst_ref=out_dst(a, head),
+            send_sem=out_send.at[a, dx, part], recv_sem=out_recv.at[a, dx, core],
+            device_id=dev, device_id_type=MESH)
 
     def given(a, dx, c):
         x = (t + 4 - dx) % 4
         return pltpu.make_async_remote_copy(
-            src_ref=out_src(a, core, t), dst_ref=out_dst(a, 2 * x + c),
-            send_sem=out_send.at[a, dx, c], recv_sem=out_recv.at[a, dx, c],
-            device_id=(chip * 2 + c, x), device_id_type=MESH)
-
-    def keep(a):
-        return pltpu.make_async_copy(out_src(a, core, t), out_dst(a, head), out_own.at[a])
-
-    def give_tile(a, c):
+            src_ref=heads_out(a, 0, t) if a < 4 else fin_at(a, 0, t), dst_ref=out_dst(a, 2 * x + c),
+            send_sem=out_send.at[a, dx, 0], recv_sem=out_recv.at[a, dx, c],
+            device_id=nxt, device_id_type=MESH)
+
+    def keep(a, part):
+        src = heads_out(a, part, t) if a < 4 else fin_at(a, part, t)
+        return pltpu.make_async_copy(src, out_dst(a, head), out_own.at[a])
+
+    def give_tile(a, part):
         for dx in (2, 1, 3):
-            give(a, dx, c).start()
-
-        @pl.when(core == c)
-        def _():
-            keep(a).start()
-
-        @pl.when(core != c)
-        def _():
-            give(a, 0, c).start()
+            give(a, dx, part).start()
+        if a < 4 and part == 1:
+            give(a, 0, part).start()
+        else:
+            c = part if a >= 4 else (1 if part == 0 else 0)
+
+            @pl.when(core == c)
+            def _():
+                keep(a, part).start()
+
+            @pl.when(core != c)
+            def _():
+                give(a, 0, part).start()
 
     def backward(b, i):
         n = b * TILES + i - b
@@ -372,10 +447,6 @@
     def back(m, a):
         return hop(48 + 2 * m + a, snd.at[m, a], rcv.at[m, a], nxt if m == 3 else prv)
 
-    def ahead(a):
-        ref = obuf if a == 0 else dqbuf
-        return hop(56 + a, ref.at[1], ref.at[2], nxt)
-
     def send_back(m, i, cond):
         for a, ref in ((0, dkT), (1, dvT)):
             snd[m, a] = ref[i].astype(BF16)
@@ -384,95 +455,123 @@
             def _():
                 back(m, a).start()
 
+    def next_here(arrays):
+        @pl.when(has_next)
+        def _():
+            for a in arrays:
+                for dx in STEPS:
+                    exchanged(a, dx, 1).wait_recv()
+
+    @pl.when(has_next)
+    def _():
+        for a in range(2):
+            for dx in STEPS:
+                down(a, dx).wait_recv()
+
+    next_here((2, 3))
+
+    early(1, 5)
+
+    @pl.when(has_prev)
+    def _():
+        for a in range(2):
+            for dx in STEPS:
+                up(a, dx, 0).wait_recv()
+
+    @pl.when(first & jnp.logical_not(origin))
+    def _():
+        for a in range(2):
+            arrived_first(a)
+
+            @pl.when(has_next)
+            def _():
+                up(a, t, 0).start()
+
+    forward(1, late_tile)
+    next_here((4, 5))
+    finish(1)
+
+    @pl.when(has_next)
+    def _():
+        give_tile(0, 1)
+        give_tile(1, 1)
+
+    forward(0, late_tile)
+
+    @pl.when(has_prev2)
+    def _():
+        for a in range(2):
+            for dx in STEPS:
+                up2(a, dx).wait_recv()
+
+    forward(0, 0)
+    finish(0)
     backward(0, 0)
     send_back(0, 0, has_prev2)
-    give_tile(0, 1)
-    give_tile(1, 1)
-
-    @pl.when(has_next)
-    def _():
-        for a in range(4):
+    give_tile(0, 0)
+    give_tile(1, 0)
+
+    @pl.when(first)
+    def _():
+        for a in (2, 3, 4, 5):
             for dx in STEPS:
-                down(a, dx).wait_recv()
-
-    def late(n, carry):
-        forward(1, 5 - n)
-        return carry
-
-    lax.fori_loop(0, TILES, late, 0)
-
-    @pl.when(has_next)
-    def _():
-        for a in (4, 5):
-            for dx in STEPS:
-                down(a, dx).wait_recv()
-
-    finish(1)
-
-    @pl.when(has_next)
-    def _():
-        ahead(0).start()
-
-    turned(1)
-    backward(1, 5)
-    send_back(3, 5, has_next)
-
-    def both(n, carry):
-        backward(n, 1)
-        return carry
-
-    lax.fori_loop(0, 2, both, 0)
-    send_back(1, 1, has_prev)
-
-    def rest(n, carry):
-        backward(1, 2 + n)
-        return carry
-
-    lax.fori_loop(0, 3, rest, 0)
-    dqbuf[1] = (acc[1] * SCALE).astype(BF16)
-
-    @pl.when(has_next)
-    def _():
-        ahead(1).start()
-
-    backward(0, 2)
-    for a, ref in ((0, dkT), (1, dvT)):
-        @pl.when(has_both)
-        def _():
-            back(0, a).wait_recv()
-            snd[2, a] = (ref[2] + rcv[0, a].astype(F32)).astype(BF16)
-
-        @pl.when(last)
-        def _():
-            snd[2, a] = ref[2].astype(BF16)
-
-        @pl.when(has_prev)
-        def _():
-            back(2, a).start()
-
-    def tail(n, carry):
-        backward(0, 3 + n)
-        return carry
-
-    lax.fori_loop(0, 2, tail, 0)
-    dqbuf[0] = (acc[0] * SCALE).astype(BF16)
-    give_tile(2, 1)
-    give_tile(3, 1)
-
-    @pl.when(first)
-    def _():
+                arrived(a, dx, 0)
         forward(2, 3)
         finish(2)
         turned(2)
         backward(2, 3)
         dqbuf[2] = (acc[2] * SCALE).astype(BF16)
-
-    @pl.when(has_prev)
-    def _():
-        ahead(0).wait_recv()
-
-    give_tile(0, 0)
-    give_tile(1, 0)
+        for a in range(4):
+            give_tile(a, 2)
+
+    turned(1)
+    backward(1, 5)
+    send_back(3, 5, has_next)
+
+    def both(n, carry):
+        backward(n, 1)
+        return carry
+
+    lax.fori_loop(0, 2, both, 0)
+    send_back(1, 1, has_prev)
+
+    def both2(n, carry):
+        backward(n, 2)
+        return carry
+
+    lax.fori_loop(0, 2, both2, 0)
+    backward(1, 3)
+    for a, ref in ((0, dkT), (1, dvT)):
+        @pl.when(has_both)
+        def _():
+            back(0, a).wait_recv()
+            snd[2, a] = (ref[2] + rcv[0, a].astype(F32)).astype(BF16)
+
+        @pl.when(last)
+        def _():
+            snd[2, a] = ref[2].astype(BF16)
+
+        @pl.when(has_prev)
+        def _():
+            back(2, a).start()
+
+    backward(1, 4)
+    dqbuf[1] = (acc[1] * SCALE).astype(BF16)
+
+    @pl.when(has_next)
+    def _():
+        give_tile(2, 1)
+        give_tile(3, 1)
+
+    def tail(n, carry):
+        backward(0, 3 + n)
+        return carry
+
+    lax.fori_loop(0, 2, tail, 0)
+    dqbuf[0] = (acc[0] * SCALE).astype(BF16)
+    give_tile(2, 0)
+    give_tile(3, 0)
+
     for i in range(2):
         for a, ref in ((0, dkT), (1, dvT)):
             if i == 0:
@@ -494,19 +593,52 @@
             fin[a, i] = jnp.transpose(ref[3 + i] * (SCALE if a == 0 else 1.0)).astype(BF16)
             give_tile(4 + a, i)
 
-    @pl.when(has_prev)
-    def _():
-        ahead(1).wait_recv()
-
-    give_tile(2, 0)
-    give_tile(3, 0)
-
     for a in range(6):
         for dx, c in ALL:
             exchange(a, dx, c).wait_send()
-            give(a, dx, c).wait_send()
+        if a >= 2:
+            @pl.when(shift == 1)
+            def _():
+                exchange(a, 0, core).wait_send()
+
+    def sent(a, part, c):
+        for dx in (1, 2, 3):
+            give(a, dx, part).wait_send()
+
+        @pl.when(core != c)
+        def _():
+            give(a, 0, part).wait_send()
+
+    for a in range(6):
+        for dx, c in ALL:
             given(a, dx, c).wait_recv()
-        keep(a).wait()
+        if a < 4:
+            @pl.when(core == 1)
+            def _():
+                keep(a, 0).wait()
+
+            @pl.when((core == 0) & has_prev)
+            def _():
+                given(a, 0, core).wait_recv()
+
+            @pl.when((core == 0) & first)
+            def _():
+                keep(a, 2).wait()
+
+            sent(a, 0, 1)
+
+            @pl.when(has_next)
+            def _():
+                for dx in STEPS:
+                    give(a, dx, 1).wait_send()
+
+            @pl.when(first)
+            def _():
+                sent(a, 2, 0)
+        else:
+            keep(a, core).wait()
+            for c in range(2):
+                sent(a, c, c)
 
     @pl.when(has_next)
     def _():
@@ -515,7 +647,6 @@
                 for c in range(2):
                     up(a, dx, c).wait_send()
             back(3, a).wait_send()
-            ahead(a).wait_send()
 
     @pl.when(has_both)
     def _():
@@ -525,10 +656,9 @@
 
     @pl.when(has_prev)
     def _():
-        for a in range(6):
+        for a in range(2):
             for dx in STEPS:
                 down(a, dx).wait_send()
-        for a in range(2):
             back(1, a).wait_send()
             back(2, a).wait_send()
 
@@ -580,9 +710,9 @@
             pltpu.VMEM((4, 2, D, B), BF16),
             pltpu.VMEM((4, 2, D, B), BF16),
             pltpu.VMEM((2, 2, B, D), BF16),
-            dma(()), dma((6, 4, 2)), dma((6, 4, 2)), dma((6,)),
-            dma((58,)), dma((58,)),
-            dma((6, 4, 2)), dma((6, 4, 2)), dma((6,)),
+            dma(()), dma((6, 4, 3)), dma((6, 4, 3)), dma((6,)),
+            dma((56,)), dma((56,)),
+            dma((6, 4, 3)), dma((6, 4, 3)), dma((6,)), pltpu.SemaphoreType.REGULAR,
         ],
         compiler_params=pltpu.CompilerParams(
             collective_id=0, has_side_effects=True, vmem_limit_bytes=40 * 1024 * 1024),

time: 45.6 us -> 43.5 us (0.954)
  Pallas kernels: 44.4 us -> 42.7 us
    pallas_call x1, Pallas kernels: 43.5 us -> 41.8 us  [body(): pl.pallas_call(functools.partial(kernel, pipe), out_shape=shapes, in_spec...]
where the time goes in v4:
time: 43.5 us; the launch traced here: 43.4 us
  Pallas kernels  42.7 us (98%)
  between operations  0.64 us (1%)
    pallas_call x1, Pallas kernels, body(): pl.pallas_call(functools.partial(kernel, pipe), out_shape=shapes, in_spec...  41.8 us
    pallas_call x1, Pallas kernels, body(): pl.pallas_call(write_kernel, out_shape=shapes, in_specs=[pl.BlockSpec(mem...  0.91 us

profile of v4, /device:TPU:1, one launch (start us, length us, event | category | flops | bytes accessed | tf_op | source)
XLA Modules:
  0.0 43.4 jit_solution(6745235514878238717)
XLA Ops:
  0.6 41.8 %shard_map.84 = (bf16[64,2048]{1,0:T(8,128)(2,1)S(1)}, bf16[64,2048]{1,0:T(8,128)(2,1)S(1)}, bf16[64,1024]{1,0:T(8,128)(2,1)S(1)}, bf16[64,1024]{1,0:T(8,128)(2,1)S(1)}) custom-call(bf16[64,2048]{1,0:T(8,128)(2,1)} %q_ref.1, bf16[64,1024]{1,0:T(8,128)(2,1)} %k_ref.1, bf16[64,1024]{1,0:T(8,128)(2,1)} %v_ref.1, bf16[64,2048]{1,0:T(8,128)(2,1)} %g_ref.1, ...), custom_call_target="tpu_custom_call" | custom-call | tf_op jit(solution)/shard_map/pallas_call | solution.py:686
  42.5 0.9 %shard_map.85 = (bf16[64,2048]{1,0:T(8,128)(2,1)}, bf16[64,2048]{1,0:T(8,128)(2,1)}, bf16[64,1024]{1,0:T(8,128)(2,1)}, bf16[64,1024]{1,0:T(8,128)(2,1)}) custom-call(bf16[64,2048]{1,0:T(8,128)(2,1)S(1)} %get-tuple-element.8.refs_0_, bf16[64,2048]{1,0:T(8,128)(2,1)S(1)} %get-tuple-element.9.refs_1_, bf16[64,1024]{1,0:T(8,128)(2,1)S(1)} %get-tuple-element.10.refs_2_, ...), custom_call_target="tpu_custom_call" | custom-call | tf_op jit(solution)/shard_map/pallas_call | solution.py:720

commit v5 on v4

--- a/solution.py
+++ b/solution.py
@@ -261,8 +261,6 @@
         def _():
             mask(2, 1, 4 * chip, 0, seg_col(4 * chip))
 
-    seg_copy.wait()
-    masks()
     mrun[...] = jnp.full(mrun.shape, NEG, F32)
     lrun[...] = jnp.zeros(lrun.shape, F32)
     acc[...] = jnp.zeros(acc.shape, F32)
@@ -350,6 +348,9 @@
         for dx in STEPS:
             arrived(a, dx, 1)
 
+    seg_copy.wait()
+    masks()
+
     here(2)
     here(3)
     n_first = 1 - n_prev
@@ -541,6 +542,14 @@
 
     lax.fori_loop(0, 2, both2, 0)
     backward(1, 3)
+    backward(1, 4)
+    dqbuf[1] = (acc[1] * SCALE).astype(BF16)
+
+    @pl.when(has_next)
+    def _():
+        give_tile(2, 1)
+        give_tile(3, 1)
+
     for a, ref in ((0, dkT), (1, dvT)):
         @pl.when(has_both)
         def _():
@@ -554,14 +563,6 @@
         @pl.when(has_prev)
         def _():
             back(2, a).start()
-
-    backward(1, 4)
-    dqbuf[1] = (acc[1] * SCALE).astype(BF16)
-
-    @pl.when(has_next)
-    def _():
-        give_tile(2, 1)
-        give_tile(3, 1)
 
     def tail(n, carry):
         backward(0, 3 + n)

time: 43.5 us -> 43.6 us (level)
  no operation moved by 1% of the time
where the time goes in v5:
time: 43.6 us; the launch traced here: 43.4 us
  Pallas kernels  42.7 us (98%)
  between operations  0.64 us (1%)
    pallas_call x1, Pallas kernels, body(): pl.pallas_call(functools.partial(kernel, pipe), out_shape=shapes, in_spec...  41.8 us
    pallas_call x1, Pallas kernels, body(): pl.pallas_call(write_kernel, out_shape=shapes, in_specs=[pl.BlockSpec(mem...  0.91 us

profile of v5, /device:TPU:1, one launch (start us, length us, event | category | flops | bytes accessed | tf_op | source)
XLA Modules:
  0.0 43.4 jit_solution(4667735823559939537)
XLA Ops:
  0.6 41.8 %shard_map.84 = (bf16[64,2048]{1,0:T(8,128)(2,1)S(1)}, bf16[64,2048]{1,0:T(8,128)(2,1)S(1)}, bf16[64,1024]{1,0:T(8,128)(2,1)S(1)}, bf16[64,1024]{1,0:T(8,128)(2,1)S(1)}) custom-call(bf16[64,2048]{1,0:T(8,128)(2,1)} %q_ref.1, bf16[64,1024]{1,0:T(8,128)(2,1)} %k_ref.1, bf16[64,1024]{1,0:T(8,128)(2,1)} %v_ref.1, bf16[64,2048]{1,0:T(8,128)(2,1)} %g_ref.1, ...), custom_call_target="tpu_custom_call" | custom-call | tf_op jit(solution)/shard_map/pallas_call | solution.py:687
  42.5 0.9 %shard_map.85 = (bf16[64,2048]{1,0:T(8,128)(2,1)}, bf16[64,2048]{1,0:T(8,128)(2,1)}, bf16[64,1024]{1,0:T(8,128)(2,1)}, bf16[64,1024]{1,0:T(8,128)(2,1)}) custom-call(bf16[64,2048]{1,0:T(8,128)(2,1)S(1)} %get-tuple-element.8.refs_0_, bf16[64,2048]{1,0:T(8,128)(2,1)S(1)} %get-tuple-element.9.refs_1_, bf16[64,1024]{1,0:T(8,128)(2,1)S(1)} %get-tuple-element.10.refs_2_, ...), custom_call_target="tpu_custom_call" | custom-call | tf_op jit(solution)/shard_map/pallas_call | solution.py:721

commit v6 on v5

--- a/solution.py
+++ b/solution.py
@@ -445,8 +445,13 @@
         dkT[i] += dot_nn(qT[b], ds)
         acc[b] += dot_nn(ds, k_tile(i))
 
-    def back(m, a):
-        return hop(48 + 2 * m + a, snd.at[m, a], rcv.at[m, a], nxt if m == 3 else prv)
+    def back(m, a, half):
+        rows = pl.ds(half * 64, 64)
+        return hop(48 + 4 * m + 2 * a + half, snd.at[m, a, rows], rcv.at[m, a, rows], nxt if m == 3 else prv)
+
+    def returned(m, a):
+        for half in range(2):
+            back(m, a, half).wait_recv()
 
     def send_back(m, i, cond):
         for a, ref in ((0, dkT), (1, dvT)):
@@ -454,7 +459,8 @@
 
             @pl.when(cond)
             def _():
-                back(m, a).start()
+                for half in range(2):
+                    back(m, a, half).start()
 
     def next_here(arrays):
         @pl.when(has_next)
@@ -551,18 +557,21 @@
         give_tile(3, 1)
 
     for a, ref in ((0, dkT), (1, dvT)):
-        @pl.when(has_both)
-        def _():
-            back(0, a).wait_recv()
-            snd[2, a] = (ref[2] + rcv[0, a].astype(F32)).astype(BF16)
-
-        @pl.when(last)
-        def _():
-            snd[2, a] = ref[2].astype(BF16)
-
-        @pl.when(has_prev)
-        def _():
-            back(2, a).start()
+        for half in range(2):
+            rows = pl.ds(half * 64, 64)
+
+            @pl.when(has_both)
+            def _():
+                back(0, a, half).wait_recv()
+                snd[2, a, rows] = (ref[2, rows] + rcv[0, a, rows].astype(F32)).astype(BF16)
+
+            @pl.when(last)
+            def _():
+                snd[2, a, rows] = ref[2, rows].astype(BF16)
+
+            @pl.when(has_prev)
+            def _():
+                back(2, a, half).start()
 
     def tail(n, carry):
         backward(0, 3 + n)
@@ -578,17 +587,17 @@
             if i == 0:
                 @pl.when(has_next)
                 def _():
-                    back(1, a).wait_recv()
+                    returned(1, a)
                     ref[3] = ref[3] + rcv[1, a].astype(F32)
 
                 @pl.when(has_prev)
                 def _():
-                    back(3, a).wait_recv()
+                    returned(3, a)
                     ref[3] = ref[3] + rcv[3, a].astype(F32)
             else:
                 @pl.when(has_next)
                 def _():
-                    back(2, a).wait_recv()
+                    returned(2, a)
                     ref[4] = ref[4] + rcv[2, a].astype(F32)
 
             fin[a, i] = jnp.transpose(ref[3 + i] * (SCALE if a == 0 else 1.0)).astype(BF16)
@@ -647,7 +656,8 @@
             for dx in STEPS:
                 for c in range(2):
                     up(a, dx, c).wait_send()
-            back(3, a).wait_send()
+            for half in range(2):
+                back(3, a, half).wait_send()
 
     @pl.when(has_both)
     def _():
@@ -660,13 +670,16 @@
         for a in range(2):
             for dx in STEPS:
                 down(a, dx).wait_send()
-            back(1, a).wait_send()
-            back(2, a).wait_send()
+            for half in range(2):
+                back(1, a, half).wait_send()
+            for half in range(2):
+                back(2, a, half).wait_send()
 
     @pl.when(has_prev2)
     def _():
         for a in range(2):
-            back(0, a).wait_send()
+            for half in range(2):
+                back(0, a, half).wait_send()
 
 
 def write_kernel(*refs):
@@ -712,7 +725,7 @@
             pltpu.VMEM((4, 2, D, B), BF16),
             pltpu.VMEM((2, 2, B, D), BF16),
             dma(()), dma((6, 4, 3)), dma((6, 4, 3)), dma((6,)),
-            dma((56,)), dma((56,)),
+            dma((64,)), dma((64,)),
             dma((6, 4, 3)), dma((6, 4, 3)), dma((6,)), pltpu.SemaphoreType.REGULAR,
         ],
         compiler_params=pltpu.CompilerParams(

time: 43.6 us -> 43.7 us (level)
  no operation moved by 1% of the time
where the time goes in v6:
time: 43.7 us; the launch traced here: 43.6 us
  Pallas kernels  42.9 us (98%)
  between operations  0.64 us (1%)
    pallas_call x1, Pallas kernels, body(): pl.pallas_call(functools.partial(kernel, pipe), out_shape=shapes, in_spec...  42 us
    pallas_call x1, Pallas kernels, body(): pl.pallas_call(write_kernel, out_shape=shapes, in_specs=[pl.BlockSpec(mem...  0.91 us

profile of v6, /device:TPU:1, one launch (start us, length us, event | category | flops | bytes accessed | tf_op | source)
XLA Modules:
  0.0 43.6 jit_solution(11485627193135042835)
XLA Ops:
  0.6 42.0 %shard_map.84 = (bf16[64,2048]{1,0:T(8,128)(2,1)S(1)}, bf16[64,2048]{1,0:T(8,128)(2,1)S(1)}, bf16[64,1024]{1,0:T(8,128)(2,1)S(1)}, bf16[64,1024]{1,0:T(8,128)(2,1)S(1)}) custom-call(bf16[64,2048]{1,0:T(8,128)(2,1)} %q_ref.1, bf16[64,1024]{1,0:T(8,128)(2,1)} %k_ref.1, bf16[64,1024]{1,0:T(8,128)(2,1)} %v_ref.1, bf16[64,2048]{1,0:T(8,128)(2,1)} %g_ref.1, ...), custom_call_target="tpu_custom_call" | custom-call | tf_op jit(solution)/shard_map/pallas_call | solution.py:700
  42.6 0.9 %shard_map.85 = (bf16[64,2048]{1,0:T(8,128)(2,1)}, bf16[64,2048]{1,0:T(8,128)(2,1)}, bf16[64,1024]{1,0:T(8,128)(2,1)}, bf16[64,1024]{1,0:T(8,128)(2,1)}) custom-call(bf16[64,2048]{1,0:T(8,128)(2,1)S(1)} %get-tuple-element.8.refs_0_, bf16[64,2048]{1,0:T(8,128)(2,1)S(1)} %get-tuple-element.9.refs_1_, bf16[64,1024]{1,0:T(8,128)(2,1)S(1)} %get-tuple-element.10.refs_2_, ...), custom_call_target="tpu_custom_call" | custom-call | tf_op jit(solution)/shard_map/pallas_call | solution.py:734
